TPU v7x, 32 devices: a whole 2x2x4 slice. The times are simulated.
32 devices in a mesh: lon: 4 (over y, x), lat: 8 (over z, core).
Axes of the slice: x: 2, y: 2, z: 4, core: 2. Of those that a mesh axis runs over, the one named last changes fastest.
Arguments:
- ocean_field: bfloat16 [256, 1024, 128], P('lon', 'lat'), may hold values from -6 to 6
- wet_tiles: int32 [4, 16], P('lon', 'lat'), may hold values from 0 to 1
- conv_weight: bfloat16 [2, 7, 7, 128], replicated, may hold values from -0.875 to 0.875
- norm_gain: float32 [2, 128], replicated, may hold values from 0.1 to 1.9
- norm_bias: float32 [2, 128], replicated, may hold values from -3 to 3
- inner_weight: bfloat16 [2, 128, 256], replicated, may hold values from -0.5 to 0.5
- inner_bias: float32 [2, 256], replicated, may hold values from -3 to 3
- outer_weight: bfloat16 [2, 256, 128], replicated, may hold values from -0.375 to 0.375
- outer_bias: float32 [2, 128], replicated, may hold values from -3 to 3
Outputs:
- updated_field: bfloat16 [256, 1024, 128], P('lon', 'lat')
All inputs are finite; a program needn't handle non-finite values.
Results may differ from a plain program's by a relative error of at most 0.0069.
Values may be sent and summed in bfloat16 or wider, within the bound.
No kernel may reach another device: no remote copies, remote signals or barrier semaphores. Data moves between devices by JAX's collectives and lax.ppermute only.
A program may use at most 64 MiB of HBM per device.

v0:
```python
import functools

import jax
import jax.numpy as jnp
from jax import lax
from jax.experimental import pallas as pl
from jax.experimental.pallas import tpu as pltpu
from jax.sharding import PartitionSpec as P

PHASE_I = 8
PHASE_J = 2
SEG = 16
STRIPS = 16
LEFT = 8


def swap_segments(parts):
    parts = list(parts)
    lane = lax.broadcasted_iota(jnp.int32, parts[0].shape, 1)
    for dist in (4, 2, 1):
        low_side = (lane // (SEG * dist)) % 2 == 0
        for p in range(8):
            if p & dist:
                continue
            low, high = parts[p], parts[p + dist]
            parts[p] = jnp.where(low_side, low, pltpu.roll(high, SEG * dist, 1))
            parts[p + dist] = jnp.where(low_side, pltpu.roll(low, 128 - SEG * dist, 1), high)
    return parts


def layer_body(
    wet_ref,
    state_ref,
    top_ref,
    bottom_ref,
    west_ref,
    east_ref,
    conv_ref,
    gain_ref,
    bias_ref,
    inner_ref,
    inner_bias_ref,
    outer_ref,
    outer_bias_ref,
    out_ref,
    wide_ref,
    taps_ref,
    rows_ref,
    band_ref,
    phased_ref,
    grouped_ref,
    cells_ref,
    branch_ref,
    *,
    tile,
):
    height, width, channels = state_ref.shape
    groups = channels // SEG
    blocks = height // PHASE_I
    steps = width // STRIPS
    pairs = steps // PHASE_J
    bf16 = jnp.bfloat16
    f32 = jnp.float32

    wide_ref[0:3, LEFT : LEFT + width, :] = top_ref[...].astype(f32)
    wide_ref[height + 3 : height + 6, LEFT : LEFT + width, :] = bottom_ref[...].astype(f32)
    wide_ref[height + 6 :] = jnp.zeros((2,) + wide_ref.shape[1:], f32)
    wide_ref[0 : height + 6, LEFT - 3 : LEFT, :] = west_ref[...].astype(f32)
    wide_ref[0 : height + 6, LEFT + width : LEFT + width + 3, :] = east_ref[...].astype(f32)

    def widen(i, carry):
        for tj in range(width // tile):
            wet = wet_ref[i // tile, tj] > 0
            piece = state_ref[i, tj * tile : (tj + 1) * tile, :].astype(f32)
            wide_ref[i + 3, LEFT + tj * tile : LEFT + (tj + 1) * tile, :] = jnp.where(
                wet, piece, 0.0
            )
        return carry

    lax.fori_loop(0, height, widen, 0, unroll=4)

    taps_ref[...] = jnp.zeros(taps_ref.shape, f32)
    taps_ref[7:14, 8:15, :] = conv_ref[...].astype(f32)

    def tap_rows(q, carry):
        for half in range(2):
            parts = []
            for p in range(8):
                pi, pj = (half * 8 + p) // 2, (half * 8 + p) % 2
                parts.append(taps_ref[q - pi + 7, pl.ds(8 - pj, 8), :])
            for g, part in enumerate(swap_segments(parts)):
                rows_ref[g, q, :, half * 128 : half * 128 + 128] = part
        return carry

    lax.fori_loop(0, 2 * PHASE_I, tap_rows, 0)

    lane = lax.broadcasted_iota(jnp.int32, (SEG, 256), 1)
    own = lax.broadcasted_iota(jnp.int32, (SEG, 256), 0) == lane % SEG

    def band(gq, carry):
        g, q = gq // (2 * PHASE_I), gq % (2 * PHASE_I)
        kb, pi = q // PHASE_I, q % PHASE_I
        for r in range(8):
            ub, pj = r // 2, r % 2
            row = jnp.broadcast_to(rows_ref[g, q, r : r + 1, :], (SEG, 256))
            band_ref[g, kb * 4 + ub, pl.ds((pi * 2 + pj) * SEG, SEG), :] = jnp.where(
                own, row, 0.0
            ).astype(bf16)
        return carry

    lax.fori_loop(0, groups * 2 * PHASE_I, band, 0, unroll=2)

    def to_phases(blk, carry):
        for u in range(pairs + 3):
            for half in range(2):
                parts = []
                for p in range(8):
                    pi, pj = (half * 8 + p) // 2, (half * 8 + p) % 2
                    strip = wide_ref[
                        blk * PHASE_I + pi, pl.ds(LEFT - 3 + 2 * u + pj, STRIPS, stride=steps), :
                    ]
                    parts.append(strip.astype(bf16))
                for g, part in enumerate(swap_segments(parts)):
                    phased_ref[g, blk, u, :, half * 128 : half * 128 + 128] = part
        return carry

    lax.fori_loop(0, blocks + 1, to_phases, 0)

    def convolve(g, carry):
        slabs = []
        mats = []
        for kb in range(2):
            for ub in range(4):
                slab = phased_ref[g, kb : kb + blocks, ub : ub + pairs]
                slabs.append(slab.reshape(blocks * pairs * STRIPS, 256))
                mats.append(band_ref[g, kb * 4 + ub])
        total = jnp.dot(
            jnp.concatenate(slabs, axis=1),
            jnp.concatenate(mats, axis=0),
            preferred_element_type=f32,
        )
        grouped_ref[g] = total.astype(bf16).reshape(blocks, pairs, STRIPS, 256)
        return carry

    lax.fori_loop(0, groups, convolve, 0)

    ones = jnp.full((channels, channels), 1.0 / channels, bf16)

    def mix(blk, carry):
        for v in range(pairs):
            for half in range(2):
                parts = swap_segments(
                    [grouped_ref[g, blk, v, :, half * 128 : half * 128 + 128] for g in range(groups)]
                )
                for p in range(8):
                    pi, pj = (half * 8 + p) // 2, (half * 8 + p) % 2
                    cells_ref[pi, 2 * v + pj] = parts[p]
        for quarter in range(4):
            conv = cells_ref[2 * quarter : 2 * quarter + 2].reshape(2 * width, channels)
            mean = jnp.dot(conv, ones, preferred_element_type=f32)
            centered = conv.astype(f32) - mean
            var = jnp.dot((centered * centered).astype(bf16), ones, preferred_element_type=f32)
            normed = (
                centered * lax.rsqrt(var + 1e-06) * gain_ref[...] + bias_ref[...]
            ).astype(bf16)
            pre = jnp.dot(normed, inner_ref[...], preferred_element_type=f32) + inner_bias_ref[...]
            hidden = (pre * (0.5 + 0.5 * lax.erf(pre * 0.7071067811865476))).astype(bf16)
            branch = (
                jnp.dot(hidden, outer_ref[...], preferred_element_type=f32) + outer_bias_ref[...]
            )
            branch_ref[2 * quarter : 2 * quarter + 2] = branch.astype(bf16).astype(f32).reshape(
                2, width, channels
            )
        for pi in range(PHASE_I):
            i = blk * PHASE_I + pi
            for s in range(0, STRIPS, 2):
                wet = wet_ref[blk * PHASE_I // tile, s * steps // tile] > 0
                delta = jnp.concatenate(
                    [branch_ref[pi, pl.ds(s + k, steps, stride=STRIPS), :] for k in range(2)], axis=0
                )
                base = state_ref[i, s * steps : (s + 2) * steps, :].astype(f32)
                out_ref[i, s * steps : (s + 2) * steps, :] = jnp.where(
                    wet, base + delta, 0.0
                ).astype(bf16)
        return carry

    lax.fori_loop(0, blocks, mix, 0)


def layer_call(wet, state, top, bottom, west, east, weights, tile):
    height, width, channels = state.shape
    groups = channels // SEG
    blocks = height // PHASE_I
    steps = width // STRIPS
    pairs = steps // PHASE_J
    assert channels == 128 and steps == 8 and height % PHASE_I == 0
    vmem = pl.BlockSpec(memory_space=pltpu.VMEM)
    smem = pl.BlockSpec(memory_space=pltpu.SMEM)

    return pl.pallas_call(
        functools.partial(layer_body, tile=tile),
        out_shape=jax.ShapeDtypeStruct(state.shape, jnp.bfloat16),
        in_specs=[smem] + [vmem] * 12,
        out_specs=vmem,
        scratch_shapes=[
            pltpu.VMEM((height + 8, width + 16, channels), jnp.float32),
            pltpu.VMEM((24, 24, channels), jnp.float32),
            pltpu.VMEM((groups, 2 * PHASE_I, 8, 256), jnp.float32),
            pltpu.VMEM((groups, 8, 256, 256), jnp.bfloat16),
            pltpu.VMEM((groups, blocks + 1, pairs + 3, STRIPS, 256), jnp.bfloat16),
            pltpu.VMEM((groups, blocks, pairs, STRIPS, 256), jnp.bfloat16),
            pltpu.VMEM((PHASE_I, steps, STRIPS, channels), jnp.bfloat16),
            pltpu.VMEM((PHASE_I, width, channels), jnp.float32),
        ],
        compiler_params=pltpu.CompilerParams(vmem_limit_bytes=48 << 20),
        name="block",
    )(wet, state, top, bottom, west, east, *weights)


def shift_pair(head, tail, axis, closed):
    count = lax.axis_size(axis)
    ends = count if closed else count - 1
    before = lax.ppermute(tail, axis, [(i, (i + 1) % count) for i in range(ends)])
    after = lax.ppermute(head, axis, [((i + 1) % count, i) for i in range(ends)])
    return before, after


def per_device(
    ocean_field,
    wet_tiles,
    conv_weight,
    norm_gain,
    norm_bias,
    inner_weight,
    inner_bias,
    outer_weight,
    outer_bias,
):
    tile = ocean_field.shape[0] // wet_tiles.shape[0]
    state = ocean_field
    for layer in range(conv_weight.shape[0]):
        if layer == 0:
            cell_wet = (
                jnp.repeat(jnp.repeat(wet_tiles, tile, axis=0), tile, axis=1)[:, :, None] > 0
            )
            edges = jnp.where(cell_wet, state, jnp.zeros((), state.dtype))
        else:
            edges = state
        top, bottom = shift_pair(edges[:3], edges[-3:], "lon", True)
        west, east = shift_pair(
            jnp.concatenate([top[:, :3], edges[:, :3], bottom[:, :3]], axis=0),
            jnp.concatenate([top[:, -3:], edges[:, -3:], bottom[:, -3:]], axis=0),
            "lat",
            False,
        )
        weights = (
            conv_weight[layer],
            norm_gain[layer][None],
            norm_bias[layer][None],
            inner_weight[layer],
            inner_bias[layer][None],
            outer_weight[layer],
            outer_bias[layer][None],
        )
        state = layer_call(wet_tiles, state, top, bottom, west, east, weights, tile)
    return state


def solution(mesh):
    return jax.shard_map(
        per_device,
        mesh=mesh,
        in_specs=(P("lon", "lat", None), P("lon", "lat"), P(), P(), P(), P(), P(), P(), P()),
        out_specs=P("lon", "lat", None),
        check_vma=False,
    )
```

profile of v0, /device:TPU:1, one launch (start us, length us, event | category | flops | bytes accessed | tf_op | source)
XLA Modules:
  0.0 115.0 jit_solution(1165539861757330195)
XLA Ops:
  0.0 0.7 compare_bitcast_fusion
  0.7 0.1 broadcast_in_dim.16
  0.7 0.1 gt.19
  0.8 0.0 copy-start.7
  0.8 0.0 copy-start.8
  0.9 0.0 copy-start.6
  0.9 0.0 copy-start
  0.9 0.0 copy-start.1
  0.9 1.9 %broadcast_select_fusion = bf16[64,128,128]{2,1,0:T(8,128)(2,1)S(1)} fusion(bf16[64,128,128]{2,1,0:T(8,128)(2,1)} %state_ref.1, pred[128]{0:T(512)(128)(4,1)S(1)} %gt.19), kind=kLoop, calls=%fused_computation | loop fusion | flops 1048576 | bytes 4194432 | tf_op jit(solution)/shard_map/jit(_where)/select_n | solution.py:246
  2.9 3.0 %collective-permute-start.1 = (bf16[3,128,128]{2,1,0:T(8,128)(2,1)S(1)}, bf16[3,128,128]{2,1,0:T(8,128)(2,1)S(1)}, u32[]{:S(2)}, u32[]{:S(2)}) collective-permute-start(bf16[3,128,128]{2,1,0:T(8,128)(2,1)S(1)} %get-tuple-element.11), channel_id=1, source_target_pairs={{8,0},{16,8},{24,16},{0,24},{9,1},{17,9},{25,17},{1,25},{10,2},{18... | collective-permute-start | bytes 294920 | tf_op jit(solution)/shard_map/ppermute | solution.py:224
  5.9 0.0 collective-permute-start
  5.9 0.1 fusion.2
  6.1 1.4 %collective-permute-done.1.bottom_ref = bf16[3,128,128]{2,1,0:T(8,128)(2,1)S(1)} collective-permute-done((bf16[3,128,128]{2,1,0:T(8,128)(2,1)S(1)}, bf16[3,128,128]{2,1,0:T(8,128)(2,1)S(1)}, u32[]{:S(2)}, u32[]{:S(2)}) %collective-permute-start.1) | collective-permute-done | bytes 98336 | tf_op jit(solution)/shard_map/ppermute | solution.py:224
  7.6 2.8 %collective-permute-done.top_ref = bf16[3,128,128]{2,1,0:T(8,128)(2,1)S(1)} collective-permute-done((bf16[3,128,128]{2,1,0:T(8,128)(2,1)S(1)}, bf16[3,128,128]{2,1,0:T(8,128)(2,1)S(1)}, u32[]{:S(2)}, u32[]{:S(2)}) %collective-permute-start) | collective-permute-done | bytes 98336 | tf_op jit(solution)/shard_map/ppermute | solution.py:223
  10.4 0.1 pad_maximum_fusion
  10.4 5.1 %collective-permute-start.2 = (bf16[70,3,128]{2,1,0:T(4,128)(2,1)S(1)}, bf16[70,3,128]{2,1,0:T(4,128)(2,1)S(1)}, u32[]{:S(2)}, u32[]{:S(2)}) collective-permute-start(bf16[70,3,128]{2,1,0:T(4,128)(2,1)S(1)} %pad_maximum_fusion), channel_id=1, source_target_pairs={{0,1},{1,2},{2,3},{3,4},{4,5},{5,6},{6,7},{8,9},{9,10},{10,11},{11... | collective-permute-start | bytes 161288 | tf_op jit(solution)/shard_map/ppermute | solution.py:223
  15.6 0.1 pad_maximum_fusion.1
  15.6 1.9 %collective-permute-start.3 = (bf16[70,3,128]{2,1,0:T(4,128)(2,1)S(1)}, bf16[70,3,128]{2,1,0:T(4,128)(2,1)S(1)}, u32[]{:S(2)}, u32[]{:S(2)}) collective-permute-start(bf16[70,3,128]{2,1,0:T(4,128)(2,1)S(1)} %pad_maximum_fusion.1), channel_id=1, source_target_pairs={{1,0},{2,1},{3,2},{4,3},{5,4},{6,5},{7,6},{9,8},{10,9},{11,10},{12... | collective-permute-start | bytes 161288 | tf_op jit(solution)/shard_map/ppermute | solution.py:224
  17.6 0.0 collective-permute-done.2.west_ref
  17.6 3.7 %collective-permute-done.3.east_ref = bf16[70,3,128]{2,1,0:T(4,128)(2,1)S(1)} collective-permute-done((bf16[70,3,128]{2,1,0:T(4,128)(2,1)S(1)}, bf16[70,3,128]{2,1,0:T(4,128)(2,1)S(1)}, u32[]{:S(2)}, u32[]{:S(2)}) %collective-permute-start.3) | collective-permute-done | bytes 53792 | tf_op jit(solution)/shard_map/ppermute | solution.py:224
  21.3 38.7 %block.2.state_ref = bf16[64,128,128]{2,1,0:T(8,128)(2,1)S(1)} custom-call(s32[1,2]{1,0:T(1,128)S(1)} %copy-done.1, bf16[64,128,128]{2,1,0:T(8,128)(2,1)S(1)} %copy-done, bf16[3,128,128]{2,1,0:T(8,128)(2,1)S(1)} %collective-permute-done.top_ref, bf16[3,128,128]{2,1,0:T(8,128)(2,1)S(1)} %collective-permute-done.1.bottom_ref, ...), custom_call_target="tpu_custom_call" | custom-call | tf_op jit(solution)/shard_map/block/pallas_call | solution.py:200
  60.0 0.8 collective-permute-start.5
  60.8 0.1 fusion
  60.9 0.7 collective-permute-start.4
  61.6 3.1 %collective-permute-done.5.bottom_ref = bf16[3,128,128]{2,1,0:T(8,128)(2,1)S(1)} collective-permute-done((bf16[3,128,128]{2,1,0:T(8,128)(2,1)S(1)}, bf16[3,128,128]{2,1,0:T(8,128)(2,1)S(1)}, u32[]{:S(2)}, u32[]{:S(2)}) %collective-permute-start.5) | collective-permute-done | bytes 98336 | tf_op jit(solution)/shard_map/ppermute | solution.py:224
  64.7 0.8 collective-permute-done.4.top_ref
  65.6 0.1 pad_maximum_fusion.2
  65.6 3.6 %collective-permute-start.6 = (bf16[70,3,128]{2,1,0:T(4,128)(2,1)S(1)}, bf16[70,3,128]{2,1,0:T(4,128)(2,1)S(1)}, u32[]{:S(2)}, u32[]{:S(2)}) collective-permute-start(bf16[70,3,128]{2,1,0:T(4,128)(2,1)S(1)} %pad_maximum_fusion.2), channel_id=1, source_target_pairs={{0,1},{1,2},{2,3},{3,4},{4,5},{5,6},{6,7},{8,9},{9,10},{10,11},{11... | collective-permute-start | bytes 161288 | tf_op jit(solution)/shard_map/ppermute | solution.py:223
  69.2 0.1 pad_maximum_fusion.3
  69.3 1.9 %collective-permute-start.7 = (bf16[70,3,128]{2,1,0:T(4,128)(2,1)S(1)}, bf16[70,3,128]{2,1,0:T(4,128)(2,1)S(1)}, u32[]{:S(2)}, u32[]{:S(2)}) collective-permute-start(bf16[70,3,128]{2,1,0:T(4,128)(2,1)S(1)} %pad_maximum_fusion.3), channel_id=1, source_target_pairs={{1,0},{2,1},{3,2},{4,3},{5,4},{6,5},{7,6},{9,8},{10,9},{11,10},{12... | collective-permute-start | bytes 161288 | tf_op jit(solution)/shard_map/ppermute | solution.py:224
  71.3 3.7 %collective-permute-done.7.east_ref = bf16[70,3,128]{2,1,0:T(4,128)(2,1)S(1)} collective-permute-done((bf16[70,3,128]{2,1,0:T(4,128)(2,1)S(1)}, bf16[70,3,128]{2,1,0:T(4,128)(2,1)S(1)}, u32[]{:S(2)}, u32[]{:S(2)}) %collective-permute-start.7) | collective-permute-done | bytes 53792 | tf_op jit(solution)/shard_map/ppermute | solution.py:224
  75.0 40.0 %block.3 = bf16[64,128,128]{2,1,0:T(8,128)(2,1)} custom-call(s32[1,2]{1,0:T(1,128)S(1)} %copy-done.1, bf16[64,128,128]{2,1,0:T(8,128)(2,1)S(1)} %block.2.state_ref, bf16[3,128,128]{2,1,0:T(8,128)(2,1)S(1)} %collective-permute-done.4.top_ref, bf16[3,128,128]{2,1,0:T(8,128)(2,1)S(1)} %collective-permute-done.5.bottom_ref, ...), custom_call_target="tpu_custom_call" | custom-call | tf_op jit(solution)/shard_map/block/pallas_call | solution.py:200
  (28 shorter events, 0.2 us)
Async XLA Ops:
  0.8 5.2 %copy-start.5 = (f32[2,256]{1,0:T(2,128)S(1)}, f32[2,256]{1,0:T(2,128)}, u32[]{:S(2)}) copy-start(f32[2,256]{1,0:T(2,128)} %param.15) | copy-start | bytes 6148
  0.8 5.2 %copy-start.4 = (bf16[2,7,7,128]{3,0,2,1:T(2,128)(2,1)S(1)}, bf16[2,7,7,128]{3,0,2,1:T(2,128)(2,1)}, u32[]{:S(2)}) copy-start(bf16[2,7,7,128]{3,0,2,1:T(2,128)(2,1)} %param.11) | copy-start | bytes 75268
  0.8 5.2 %copy-start.2 = (bf16[2,128,256]{2,1,0:T(8,128)(2,1)S(1)}, bf16[2,128,256]{2,1,0:T(8,128)(2,1)}, u32[]{:S(2)}) copy-start(bf16[2,128,256]{2,1,0:T(8,128)(2,1)} %param.14) | copy-start | bytes 393220
  0.8 5.3 %copy-start.3 = (bf16[2,256,128]{2,1,0:T(8,128)(2,1)S(1)}, bf16[2,256,128]{2,1,0:T(8,128)(2,1)}, u32[]{:S(2)}) copy-start(bf16[2,256,128]{2,1,0:T(8,128)(2,1)} %param.16) | copy-start | bytes 393220
  0.8 5.3 %copy-start.7 = (f32[2,128]{1,0:T(2,128)S(1)}, f32[2,128]{1,0:T(2,128)}, u32[]{:S(2)}) copy-start(f32[2,128]{1,0:T(2,128)} %param.17) | copy-start | bytes 3076
  0.8 5.3 %copy-start.8 = (f32[2,128]{1,0:T(2,128)S(1)}, f32[2,128]{1,0:T(2,128)}, u32[]{:S(2)}) copy-start(f32[2,128]{1,0:T(2,128)} %param.13) | copy-start | bytes 3076
  0.9 16.7 %copy-start.6 = (f32[2,128]{1,0:T(2,128)S(1)}, f32[2,128]{1,0:T(2,128)}, u32[]{:S(2)}) copy-start(f32[2,128]{1,0:T(2,128)} %param.12) | copy-start | bytes 3076
  0.9 20.4 %copy-start = (bf16[64,128,128]{2,1,0:T(8,128)(2,1)S(1)}, bf16[64,128,128]{2,1,0:T(8,128)(2,1)}, u32[]{:S(2)}) copy-start(bf16[64,128,128]{2,1,0:T(8,128)(2,1)} %state_ref.1) | copy-start | bytes 6291460
  0.9 20.4 %copy-start.1 = (s32[1,2]{1,0:T(1,128)S(1)}, s32[1,2]{1,0:T(1,128)}, u32[]{:S(2)}) copy-start(s32[1,2]{1,0:T(1,128)} %wet_ref.3) | copy-start | bytes 28
  2.9 4.7 %collective-permute-start.1 = (bf16[3,128,128]{2,1,0:T(8,128)(2,1)S(1)}, bf16[3,128,128]{2,1,0:T(8,128)(2,1)S(1)}, u32[]{:S(2)}, u32[]{:S(2)}) collective-permute-start(bf16[3,128,128]{2,1,0:T(8,128)(2,1)S(1)} %get-tuple-element.11), channel_id=1, source_target_pairs={{8,0},{16,8},{24,16},{0,24},{9,1},{17,9},{25,17},{1,25},{10,2},{18... | collective-permute-start | bytes 294920 | tf_op jit(solution)/shard_map/ppermute | solution.py:224
  5.9 4.4 %collective-permute-start = (bf16[3,128,128]{2,1,0:T(8,128)(2,1)S(1)}, bf16[3,128,128]{2,1,0:T(8,128)(2,1)S(1)}, u32[]{:S(2)}, u32[]{:S(2)}) collective-permute-start(bf16[3,128,128]{2,1,0:T(8,128)(2,1)S(1)} %get-tuple-element.12), channel_id=1, source_target_pairs={{0,8},{8,16},{16,24},{24,0},{1,9},{9,17},{17,25},{25,1},{2,10},{10... | collective-permute-start | bytes 294920 | tf_op jit(solution)/shard_map/ppermute | solution.py:223
  10.4 7.2 %collective-permute-start.2 = (bf16[70,3,128]{2,1,0:T(4,128)(2,1)S(1)}, bf16[70,3,128]{2,1,0:T(4,128)(2,1)S(1)}, u32[]{:S(2)}, u32[]{:S(2)}) collective-permute-start(bf16[70,3,128]{2,1,0:T(4,128)(2,1)S(1)} %pad_maximum_fusion), channel_id=1, source_target_pairs={{0,1},{1,2},{2,3},{3,4},{4,5},{5,6},{6,7},{8,9},{9,10},{10,11},{11... | collective-permute-start | bytes 161288 | tf_op jit(solution)/shard_map/ppermute | solution.py:223
  15.6 5.7 %collective-permute-start.3 = (bf16[70,3,128]{2,1,0:T(4,128)(2,1)S(1)}, bf16[70,3,128]{2,1,0:T(4,128)(2,1)S(1)}, u32[]{:S(2)}, u32[]{:S(2)}) collective-permute-start(bf16[70,3,128]{2,1,0:T(4,128)(2,1)S(1)} %pad_maximum_fusion.1), channel_id=1, source_target_pairs={{1,0},{2,1},{3,2},{4,3},{5,4},{6,5},{7,6},{9,8},{10,9},{11,10},{12... | collective-permute-start | bytes 161288 | tf_op jit(solution)/shard_map/ppermute | solution.py:224
  60.0 4.8 %collective-permute-start.5 = (bf16[3,128,128]{2,1,0:T(8,128)(2,1)S(1)}, bf16[3,128,128]{2,1,0:T(8,128)(2,1)S(1)}, u32[]{:S(2)}, u32[]{:S(2)}) collective-permute-start(bf16[3,128,128]{2,1,0:T(8,128)(2,1)S(1)} %get-tuple-element.7), channel_id=1, source_target_pairs={{8,0},{16,8},{24,16},{0,24},{9,1},{17,9},{25,17},{1,25},{10,2},{18... | collective-permute-start | bytes 294920 | tf_op jit(solution)/shard_map/ppermute | solution.py:224
  60.9 4.7 %collective-permute-start.4 = (bf16[3,128,128]{2,1,0:T(8,128)(2,1)S(1)}, bf16[3,128,128]{2,1,0:T(8,128)(2,1)S(1)}, u32[]{:S(2)}, u32[]{:S(2)}) collective-permute-start(bf16[3,128,128]{2,1,0:T(8,128)(2,1)S(1)} %get-tuple-element.8), channel_id=1, source_target_pairs={{0,8},{8,16},{16,24},{24,0},{1,9},{9,17},{17,25},{25,1},{2,10},{10... | collective-permute-start | bytes 294920 | tf_op jit(solution)/shard_map/ppermute | solution.py:223
  65.6 5.6 %collective-permute-start.6 = (bf16[70,3,128]{2,1,0:T(4,128)(2,1)S(1)}, bf16[70,3,128]{2,1,0:T(4,128)(2,1)S(1)}, u32[]{:S(2)}, u32[]{:S(2)}) collective-permute-start(bf16[70,3,128]{2,1,0:T(4,128)(2,1)S(1)} %pad_maximum_fusion.2), channel_id=1, source_target_pairs={{0,1},{1,2},{2,3},{3,4},{4,5},{5,6},{6,7},{8,9},{9,10},{10,11},{11... | collective-permute-start | bytes 161288 | tf_op jit(solution)/shard_map/ppermute | solution.py:223
  69.3 5.7 %collective-permute-start.7 = (bf16[70,3,128]{2,1,0:T(4,128)(2,1)S(1)}, bf16[70,3,128]{2,1,0:T(4,128)(2,1)S(1)}, u32[]{:S(2)}, u32[]{:S(2)}) collective-permute-start(bf16[70,3,128]{2,1,0:T(4,128)(2,1)S(1)} %pad_maximum_fusion.3), channel_id=1, source_target_pairs={{1,0},{2,1},{3,2},{4,3},{5,4},{6,5},{7,6},{9,8},{10,9},{11,10},{12... | collective-permute-start | bytes 161288 | tf_op jit(solution)/shard_map/ppermute | solution.py:224
where the time goes:
time: 115 us
  Pallas kernels  78.7 us (68%)
  starting transfers between devices  17.2 us (15%)
  waiting for transfers between devices  15.5 us (13%)
  other arithmetic  2.84 us (2%)
    pallas_call x2, Pallas kernels, layer_call(): pl.pallas_call(functools.partial(layer_body, tile=tile), out_shape=jax.Sh...  78.7 us
    ppermute x4, waiting for transfers between devices, shift_pair(): lax.ppermute(head, axis, [((i + 1) % count, i) for i in range(ends)])  11.9 us
    ppermute x4, starting transfers between devices, shift_pair(): lax.ppermute(tail, axis, [(i, (i + 1) % count) for i in range(ends)])  9.45 us
    ppermute x4, starting transfers between devices, shift_pair(): lax.ppermute(head, axis, [((i + 1) % count, i) for i in range(ends)])  7.72 us
    ppermute x4, waiting for transfers between devices, shift_pair(): lax.ppermute(tail, axis, [(i, (i + 1) % count) for i in range(ends)])  3.61 us
  transfers between devices with their start and end apart: 8, of which 6 were waited for; matrix products, arithmetic and copies ran while one was open for 0% of the time, Pallas kernels for 0%

commit v1 on v0

--- a/solution.py
+++ b/solution.py
@@ -12,20 +12,29 @@
 SEG = 16
 STRIPS = 16
 LEFT = 8
-
-
-def swap_segments(parts):
+ROWS = 8
+
+
+def swap_segments(parts, back=False):
     parts = list(parts)
     lane = lax.broadcasted_iota(jnp.int32, parts[0].shape, 1)
-    for dist in (4, 2, 1):
+    for dist in (1, 2, 4) if back else (4, 2, 1):
         low_side = (lane // (SEG * dist)) % 2 == 0
+        turn = 128 - SEG * dist if back else SEG * dist
         for p in range(8):
             if p & dist:
                 continue
             low, high = parts[p], parts[p + dist]
-            parts[p] = jnp.where(low_side, low, pltpu.roll(high, SEG * dist, 1))
-            parts[p + dist] = jnp.where(low_side, pltpu.roll(low, 128 - SEG * dist, 1), high)
+            moved = pltpu.roll(jnp.where(low_side, high, low), turn, 1)
+            parts[p] = jnp.where(low_side, low, moved)
+            parts[p + dist] = jnp.where(low_side, moved, high)
     return parts
+
+
+def lane_slot(g, p):
+    p1, p2, p4 = p & 1, p >> 1 & 1, p >> 2 & 1
+    high = p4 ^ ((g >> 1) & (1 - p2))
+    return ((high * 2 + p2 + (g & (1 - p1))) & 3) * 2 + p1
 
 
 def layer_body(
@@ -51,6 +60,8 @@
     grouped_ref,
     cells_ref,
     branch_ref,
+    average_ref,
+    center_ref,
     *,
     tile,
 ):
@@ -97,18 +108,19 @@
     lane = lax.broadcasted_iota(jnp.int32, (SEG, 256), 1)
     own = lax.broadcasted_iota(jnp.int32, (SEG, 256), 0) == lane % SEG
 
-    def band(gq, carry):
-        g, q = gq // (2 * PHASE_I), gq % (2 * PHASE_I)
-        kb, pi = q // PHASE_I, q % PHASE_I
-        for r in range(8):
-            ub, pj = r // 2, r % 2
-            row = jnp.broadcast_to(rows_ref[g, q, r : r + 1, :], (SEG, 256))
-            band_ref[g, kb * 4 + ub, pl.ds((pi * 2 + pj) * SEG, SEG), :] = jnp.where(
-                own, row, 0.0
-            ).astype(bf16)
-        return carry
-
-    lax.fori_loop(0, groups * 2 * PHASE_I, band, 0, unroll=2)
+    def band(step, carry):
+        g, kb = step >> 1, step & 1
+        for p in range(16):
+            slot = (p >> 3) * 8 + lane_slot(g, p & 7)
+            for ub in range(4):
+                r = 2 * ub + (p & 1)
+                row = rows_ref[g, kb * PHASE_I + (p >> 1), r : r + 1, :]
+                band_ref[g, kb * 4 + ub, pl.ds(pl.multiple_of(slot * SEG, SEG), SEG), :] = jnp.where(
+                    own, jnp.broadcast_to(row, (SEG, 256)), 0.0
+                ).astype(bf16)
+        return carry
+
+    lax.fori_loop(0, groups * 2, band, 0)
 
     def to_phases(blk, carry):
         for u in range(pairs + 3):
@@ -144,33 +156,52 @@
 
     lax.fori_loop(0, groups, convolve, 0)
 
-    ones = jnp.full((channels, channels), 1.0 / channels, bf16)
+    row = lax.broadcasted_iota(jnp.int32, (256, 256), 0)
+    col = lax.broadcasted_iota(jnp.int32, (256, 256), 1)
+    share = jnp.where(row // channels == col // channels, 1.0 / channels, 0.0)
+    average_ref[...] = share.astype(bf16)
+    center_ref[...] = (jnp.where(row == col, 1.0, 0.0) - share).astype(bf16)
 
     def mix(blk, carry):
         for v in range(pairs):
             for half in range(2):
                 parts = swap_segments(
-                    [grouped_ref[g, blk, v, :, half * 128 : half * 128 + 128] for g in range(groups)]
+                    [grouped_ref[g, blk, v, :, half * 128 : half * 128 + 128] for g in range(groups)],
+                    back=True,
                 )
                 for p in range(8):
                     pi, pj = (half * 8 + p) // 2, (half * 8 + p) % 2
-                    cells_ref[pi, 2 * v + pj] = parts[p]
-        for quarter in range(4):
-            conv = cells_ref[2 * quarter : 2 * quarter + 2].reshape(2 * width, channels)
-            mean = jnp.dot(conv, ones, preferred_element_type=f32)
-            centered = conv.astype(f32) - mean
-            var = jnp.dot((centered * centered).astype(bf16), ones, preferred_element_type=f32)
+                    cells_ref[pi, v, :, pj * channels : (pj + 1) * channels] = parts[p]
+        for part in range(PHASE_I // ROWS):
+            first = part * ROWS
+            count = ROWS * pairs * STRIPS
+            conv = cells_ref[first : first + ROWS].reshape(count, 2 * channels)
+            centered = jnp.dot(conv, center_ref[...], preferred_element_type=f32)
+            var = jnp.dot(
+                (centered * centered).astype(bf16), average_ref[...], preferred_element_type=f32
+            )
             normed = (
                 centered * lax.rsqrt(var + 1e-06) * gain_ref[...] + bias_ref[...]
             ).astype(bf16)
-            pre = jnp.dot(normed, inner_ref[...], preferred_element_type=f32) + inner_bias_ref[...]
-            hidden = (pre * (0.5 + 0.5 * lax.erf(pre * 0.7071067811865476))).astype(bf16)
-            branch = (
-                jnp.dot(hidden, outer_ref[...], preferred_element_type=f32) + outer_bias_ref[...]
-            )
-            branch_ref[2 * quarter : 2 * quarter + 2] = branch.astype(bf16).astype(f32).reshape(
-                2, width, channels
-            )
+            for pj in range(PHASE_J):
+                pre = (
+                    jnp.dot(
+                        normed[:, pj * channels : (pj + 1) * channels],
+                        inner_ref[...],
+                        preferred_element_type=f32,
+                    )
+                    + inner_bias_ref[...]
+                )
+                hidden = (pre * (0.5 + 0.5 * lax.erf(pre * 0.7071067811865476))).astype(bf16)
+                branch = (
+                    jnp.dot(hidden, outer_ref[...], preferred_element_type=f32)
+                    + outer_bias_ref[...]
+                )
+                branch = branch.astype(bf16).astype(f32).reshape(ROWS, pairs, STRIPS, channels)
+                for pi in range(ROWS):
+                    for v in range(pairs):
+                        start = (2 * v + pj) * STRIPS
+                        branch_ref[first + pi, start : start + STRIPS, :] = branch[pi, v]
         for pi in range(PHASE_I):
             i = blk * PHASE_I + pi
             for s in range(0, STRIPS, 2):
@@ -209,8 +240,10 @@
             pltpu.VMEM((groups, 8, 256, 256), jnp.bfloat16),
             pltpu.VMEM((groups, blocks + 1, pairs + 3, STRIPS, 256), jnp.bfloat16),
             pltpu.VMEM((groups, blocks, pairs, STRIPS, 256), jnp.bfloat16),
-            pltpu.VMEM((PHASE_I, steps, STRIPS, channels), jnp.bfloat16),
+            pltpu.VMEM((PHASE_I, pairs, STRIPS, 2 * channels), jnp.bfloat16),
             pltpu.VMEM((PHASE_I, width, channels), jnp.float32),
+            pltpu.VMEM((256, 256), jnp.bfloat16),
+            pltpu.VMEM((256, 256), jnp.bfloat16),
         ],
         compiler_params=pltpu.CompilerParams(vmem_limit_bytes=48 << 20),
         name="block",
@@ -255,8 +288,8 @@
         )
         weights = (
             conv_weight[layer],
-            norm_gain[layer][None],
-            norm_bias[layer][None],
+            jnp.tile(norm_gain[layer][None], (1, 2)),
+            jnp.tile(norm_bias[layer][None], (1, 2)),
             inner_weight[layer],
             inner_bias[layer][None],
             outer_weight[layer],

time: 115 us -> 87.1 us (0.76)
  Pallas kernels: 78.7 us -> 50.6 us
    pallas_call x2, Pallas kernels: 78.7 us -> 50.6 us  [layer_call(): pl.pallas_call(functools.partial(layer_body, tile=tile), out_shape=jax.Sh...]
where the time goes in v1:
time: 87.1 us; the launch traced here: 86.9 us
  Pallas kernels  50.6 us (58%)
  starting transfers between devices  17.2 us (20%)
  waiting for transfers between devices  15.5 us (18%)
  other arithmetic  2.84 us (3%)
    pallas_call x2, Pallas kernels, layer_call(): pl.pallas_call(functools.partial(layer_body, tile=tile), out_shape=jax.Sh...  50.6 us
    ppermute x4, waiting for transfers between devices, shift_pair(): lax.ppermute(head, axis, [((i + 1) % count, i) for i in range(ends)])  11.9 us
    ppermute x4, starting transfers between devices, shift_pair(): lax.ppermute(tail, axis, [(i, (i + 1) % count) for i in range(ends)])  9.45 us
    ppermute x4, starting transfers between devices, shift_pair(): lax.ppermute(head, axis, [((i + 1) % count, i) for i in range(ends)])  7.72 us
    ppermute x4, waiting for transfers between devices, shift_pair(): lax.ppermute(tail, axis, [(i, (i + 1) % count) for i in range(ends)])  3.61 us
    select_n x1, other arithmetic, per_device(): edges = jnp.where(cell_wet, state, jnp.zeros((), state.dtype))  1.95 us
  transfers between devices with their start and end apart: 8, of which 6 were waited for; matrix products, arithmetic and copies ran while one was open for 0% of the time, Pallas kernels for 0%

profile of v1, /device:TPU:1, one launch (start us, length us, event | category | flops | bytes accessed | tf_op | source)
XLA Modules:
  0.0 86.9 jit_solution(16162753301918872101)
XLA Ops:
  0.0 0.7 compare_bitcast_fusion
  0.7 0.1 broadcast_in_dim.16
  0.7 0.1 gt.19
  0.8 0.0 copy-start.3
  0.8 0.0 copy-start.7
  0.9 0.0 copy-start.8
  0.9 0.0 copy-start
  0.9 0.0 copy-start.1
  0.9 1.9 %broadcast_select_fusion = bf16[64,128,128]{2,1,0:T(8,128)(2,1)S(1)} fusion(bf16[64,128,128]{2,1,0:T(8,128)(2,1)} %state_ref.1, pred[128]{0:T(512)(128)(4,1)S(1)} %gt.19), kind=kLoop, calls=%fused_computation | loop fusion | flops 1048576 | bytes 4194432 | tf_op jit(solution)/shard_map/jit(_where)/select_n | solution.py:279
  2.9 3.0 %collective-permute-start.1 = (bf16[3,128,128]{2,1,0:T(8,128)(2,1)S(1)}, bf16[3,128,128]{2,1,0:T(8,128)(2,1)S(1)}, u32[]{:S(2)}, u32[]{:S(2)}) collective-permute-start(bf16[3,128,128]{2,1,0:T(8,128)(2,1)S(1)} %get-tuple-element.11), channel_id=1, source_target_pairs={{8,0},{16,8},{24,16},{0,24},{9,1},{17,9},{25,17},{1,25},{10,2},{18... | collective-permute-start | bytes 294920 | tf_op jit(solution)/shard_map/ppermute | solution.py:257
  5.9 0.0 collective-permute-start
  5.9 0.1 fusion.2
  6.2 1.4 %collective-permute-done.1.bottom_ref = bf16[3,128,128]{2,1,0:T(8,128)(2,1)S(1)} collective-permute-done((bf16[3,128,128]{2,1,0:T(8,128)(2,1)S(1)}, bf16[3,128,128]{2,1,0:T(8,128)(2,1)S(1)}, u32[]{:S(2)}, u32[]{:S(2)}) %collective-permute-start.1) | collective-permute-done | bytes 98336 | tf_op jit(solution)/shard_map/ppermute | solution.py:257
  7.6 2.8 %collective-permute-done.top_ref = bf16[3,128,128]{2,1,0:T(8,128)(2,1)S(1)} collective-permute-done((bf16[3,128,128]{2,1,0:T(8,128)(2,1)S(1)}, bf16[3,128,128]{2,1,0:T(8,128)(2,1)S(1)}, u32[]{:S(2)}, u32[]{:S(2)}) %collective-permute-start) | collective-permute-done | bytes 98336 | tf_op jit(solution)/shard_map/ppermute | solution.py:256
  10.4 0.1 pad_maximum_fusion
  10.4 5.1 %collective-permute-start.2 = (bf16[70,3,128]{2,1,0:T(4,128)(2,1)S(1)}, bf16[70,3,128]{2,1,0:T(4,128)(2,1)S(1)}, u32[]{:S(2)}, u32[]{:S(2)}) collective-permute-start(bf16[70,3,128]{2,1,0:T(4,128)(2,1)S(1)} %pad_maximum_fusion), channel_id=1, source_target_pairs={{0,1},{1,2},{2,3},{3,4},{4,5},{5,6},{6,7},{8,9},{9,10},{10,11},{11... | collective-permute-start | bytes 161288 | tf_op jit(solution)/shard_map/ppermute | solution.py:256
  15.6 0.1 pad_maximum_fusion.1
  15.6 1.9 %collective-permute-start.3 = (bf16[70,3,128]{2,1,0:T(4,128)(2,1)S(1)}, bf16[70,3,128]{2,1,0:T(4,128)(2,1)S(1)}, u32[]{:S(2)}, u32[]{:S(2)}) collective-permute-start(bf16[70,3,128]{2,1,0:T(4,128)(2,1)S(1)} %pad_maximum_fusion.1), channel_id=1, source_target_pairs={{1,0},{2,1},{3,2},{4,3},{5,4},{6,5},{7,6},{9,8},{10,9},{11,10},{12... | collective-permute-start | bytes 161288 | tf_op jit(solution)/shard_map/ppermute | solution.py:257
  17.6 3.7 %collective-permute-done.3.east_ref = bf16[70,3,128]{2,1,0:T(4,128)(2,1)S(1)} collective-permute-done((bf16[70,3,128]{2,1,0:T(4,128)(2,1)S(1)}, bf16[70,3,128]{2,1,0:T(4,128)(2,1)S(1)}, u32[]{:S(2)}, u32[]{:S(2)}) %collective-permute-start.3) | collective-permute-done | bytes 53792 | tf_op jit(solution)/shard_map/ppermute | solution.py:257
  21.3 24.6 %block.2.state_ref = bf16[64,128,128]{2,1,0:T(8,128)(2,1)S(1)} custom-call(s32[1,2]{1,0:T(1,128)S(1)} %copy-done.1, bf16[64,128,128]{2,1,0:T(8,128)(2,1)S(1)} %copy-done, bf16[3,128,128]{2,1,0:T(8,128)(2,1)S(1)} %collective-permute-done.top_ref, bf16[3,128,128]{2,1,0:T(8,128)(2,1)S(1)} %collective-permute-done.1.bottom_ref, ...), custom_call_target="tpu_custom_call" | custom-call | tf_op jit(solution)/shard_map/block/pallas_call | solution.py:231
  45.9 0.8 collective-permute-start.5
  46.8 0.1 fusion
  46.8 0.7 collective-permute-start.4
  47.6 3.1 %collective-permute-done.5.bottom_ref = bf16[3,128,128]{2,1,0:T(8,128)(2,1)S(1)} collective-permute-done((bf16[3,128,128]{2,1,0:T(8,128)(2,1)S(1)}, bf16[3,128,128]{2,1,0:T(8,128)(2,1)S(1)}, u32[]{:S(2)}, u32[]{:S(2)}) %collective-permute-start.5) | collective-permute-done | bytes 98336 | tf_op jit(solution)/shard_map/ppermute | solution.py:257
  50.7 0.8 collective-permute-done.4.top_ref
  51.5 0.1 pad_maximum_fusion.2
  51.6 3.6 %collective-permute-start.6 = (bf16[70,3,128]{2,1,0:T(4,128)(2,1)S(1)}, bf16[70,3,128]{2,1,0:T(4,128)(2,1)S(1)}, u32[]{:S(2)}, u32[]{:S(2)}) collective-permute-start(bf16[70,3,128]{2,1,0:T(4,128)(2,1)S(1)} %pad_maximum_fusion.2), channel_id=1, source_target_pairs={{0,1},{1,2},{2,3},{3,4},{4,5},{5,6},{6,7},{8,9},{9,10},{10,11},{11... | collective-permute-start | bytes 161288 | tf_op jit(solution)/shard_map/ppermute | solution.py:256
  55.2 0.1 pad_maximum_fusion.3
  55.3 1.9 %collective-permute-start.7 = (bf16[70,3,128]{2,1,0:T(4,128)(2,1)S(1)}, bf16[70,3,128]{2,1,0:T(4,128)(2,1)S(1)}, u32[]{:S(2)}, u32[]{:S(2)}) collective-permute-start(bf16[70,3,128]{2,1,0:T(4,128)(2,1)S(1)} %pad_maximum_fusion.3), channel_id=1, source_target_pairs={{1,0},{2,1},{3,2},{4,3},{5,4},{6,5},{7,6},{9,8},{10,9},{11,10},{12... | collective-permute-start | bytes 161288 | tf_op jit(solution)/shard_map/ppermute | solution.py:257
  57.2 0.0 collective-permute-done.6.west_ref
  57.2 3.7 %collective-permute-done.7.east_ref = bf16[70,3,128]{2,1,0:T(4,128)(2,1)S(1)} collective-permute-done((bf16[70,3,128]{2,1,0:T(4,128)(2,1)S(1)}, bf16[70,3,128]{2,1,0:T(4,128)(2,1)S(1)}, u32[]{:S(2)}, u32[]{:S(2)}) %collective-permute-start.7) | collective-permute-done | bytes 53792 | tf_op jit(solution)/shard_map/ppermute | solution.py:257
  60.9 26.0 %block.3 = bf16[64,128,128]{2,1,0:T(8,128)(2,1)} custom-call(s32[1,2]{1,0:T(1,128)S(1)} %copy-done.1, bf16[64,128,128]{2,1,0:T(8,128)(2,1)S(1)} %block.2.state_ref, bf16[3,128,128]{2,1,0:T(8,128)(2,1)S(1)} %collective-permute-done.4.top_ref, bf16[3,128,128]{2,1,0:T(8,128)(2,1)S(1)} %collective-permute-done.5.bottom_ref, ...), custom_call_target="tpu_custom_call" | custom-call | tf_op jit(solution)/shard_map/block/pallas_call | solution.py:231
  (33 shorter events, 0.2 us)
Async XLA Ops:
  0.8 5.2 %copy-start.6 = (f32[2,128]{1,0:T(2,128)S(1)}, f32[2,128]{1,0:T(2,128)}, u32[]{:S(2)}) copy-start(f32[2,128]{1,0:T(2,128)} %param.12) | copy-start | bytes 3076
  0.8 5.2 %copy-start.5 = (f32[2,256]{1,0:T(2,128)S(1)}, f32[2,256]{1,0:T(2,128)}, u32[]{:S(2)}) copy-start(f32[2,256]{1,0:T(2,128)} %param.15) | copy-start | bytes 6148
  0.8 5.2 %copy-start.4 = (bf16[2,7,7,128]{3,0,2,1:T(2,128)(2,1)S(1)}, bf16[2,7,7,128]{3,0,2,1:T(2,128)(2,1)}, u32[]{:S(2)}) copy-start(bf16[2,7,7,128]{3,0,2,1:T(2,128)(2,1)} %param.11) | copy-start | bytes 75268
  0.8 5.2 %copy-start.2 = (bf16[2,128,256]{2,1,0:T(8,128)(2,1)S(1)}, bf16[2,128,256]{2,1,0:T(8,128)(2,1)}, u32[]{:S(2)}) copy-start(bf16[2,128,256]{2,1,0:T(8,128)(2,1)} %param.14) | copy-start | bytes 393220
  0.8 5.3 %copy-start.3 = (bf16[2,256,128]{2,1,0:T(8,128)(2,1)S(1)}, bf16[2,256,128]{2,1,0:T(8,128)(2,1)}, u32[]{:S(2)}) copy-start(bf16[2,256,128]{2,1,0:T(8,128)(2,1)} %param.16) | copy-start | bytes 393220
  0.8 5.3 %copy-start.7 = (f32[2,128]{1,0:T(2,128)S(1)}, f32[2,128]{1,0:T(2,128)}, u32[]{:S(2)}) copy-start(f32[2,128]{1,0:T(2,128)} %param.13) | copy-start | bytes 3076
  0.9 16.7 %copy-start.8 = (f32[2,128]{1,0:T(2,128)S(1)}, f32[2,128]{1,0:T(2,128)}, u32[]{:S(2)}) copy-start(f32[2,128]{1,0:T(2,128)} %param.17) | copy-start | bytes 3076
  0.9 20.4 %copy-start = (bf16[64,128,128]{2,1,0:T(8,128)(2,1)S(1)}, bf16[64,128,128]{2,1,0:T(8,128)(2,1)}, u32[]{:S(2)}) copy-start(bf16[64,128,128]{2,1,0:T(8,128)(2,1)} %state_ref.1) | copy-start | bytes 6291460
  0.9 20.4 %copy-start.1 = (s32[1,2]{1,0:T(1,128)S(1)}, s32[1,2]{1,0:T(1,128)}, u32[]{:S(2)}) copy-start(s32[1,2]{1,0:T(1,128)} %wet_ref.3) | copy-start | bytes 28
  2.9 4.7 %collective-permute-start.1 = (bf16[3,128,128]{2,1,0:T(8,128)(2,1)S(1)}, bf16[3,128,128]{2,1,0:T(8,128)(2,1)S(1)}, u32[]{:S(2)}, u32[]{:S(2)}) collective-permute-start(bf16[3,128,128]{2,1,0:T(8,128)(2,1)S(1)} %get-tuple-element.11), channel_id=1, source_target_pairs={{8,0},{16,8},{24,16},{0,24},{9,1},{17,9},{25,17},{1,25},{10,2},{18... | collective-permute-start | bytes 294920 | tf_op jit(solution)/shard_map/ppermute | solution.py:257
  5.9 4.4 %collective-permute-start = (bf16[3,128,128]{2,1,0:T(8,128)(2,1)S(1)}, bf16[3,128,128]{2,1,0:T(8,128)(2,1)S(1)}, u32[]{:S(2)}, u32[]{:S(2)}) collective-permute-start(bf16[3,128,128]{2,1,0:T(8,128)(2,1)S(1)} %get-tuple-element.12), channel_id=1, source_target_pairs={{0,8},{8,16},{16,24},{24,0},{1,9},{9,17},{17,25},{25,1},{2,10},{10... | collective-permute-start | bytes 294920 | tf_op jit(solution)/shard_map/ppermute | solution.py:256
  10.4 7.2 %collective-permute-start.2 = (bf16[70,3,128]{2,1,0:T(4,128)(2,1)S(1)}, bf16[70,3,128]{2,1,0:T(4,128)(2,1)S(1)}, u32[]{:S(2)}, u32[]{:S(2)}) collective-permute-start(bf16[70,3,128]{2,1,0:T(4,128)(2,1)S(1)} %pad_maximum_fusion), channel_id=1, source_target_pairs={{0,1},{1,2},{2,3},{3,4},{4,5},{5,6},{6,7},{8,9},{9,10},{10,11},{11... | collective-permute-start | bytes 161288 | tf_op jit(solution)/shard_map/ppermute | solution.py:256
  15.6 5.7 %collective-permute-start.3 = (bf16[70,3,128]{2,1,0:T(4,128)(2,1)S(1)}, bf16[70,3,128]{2,1,0:T(4,128)(2,1)S(1)}, u32[]{:S(2)}, u32[]{:S(2)}) collective-permute-start(bf16[70,3,128]{2,1,0:T(4,128)(2,1)S(1)} %pad_maximum_fusion.1), channel_id=1, source_target_pairs={{1,0},{2,1},{3,2},{4,3},{5,4},{6,5},{7,6},{9,8},{10,9},{11,10},{12... | collective-permute-start | bytes 161288 | tf_op jit(solution)/shard_map/ppermute | solution.py:257
  45.9 4.8 %collective-permute-start.5 = (bf16[3,128,128]{2,1,0:T(8,128)(2,1)S(1)}, bf16[3,128,128]{2,1,0:T(8,128)(2,1)S(1)}, u32[]{:S(2)}, u32[]{:S(2)}) collective-permute-start(bf16[3,128,128]{2,1,0:T(8,128)(2,1)S(1)} %get-tuple-element.7), channel_id=1, source_target_pairs={{8,0},{16,8},{24,16},{0,24},{9,1},{17,9},{25,17},{1,25},{10,2},{18... | collective-permute-start | bytes 294920 | tf_op jit(solution)/shard_map/ppermute | solution.py:257
  46.8 4.7 %collective-permute-start.4 = (bf16[3,128,128]{2,1,0:T(8,128)(2,1)S(1)}, bf16[3,128,128]{2,1,0:T(8,128)(2,1)S(1)}, u32[]{:S(2)}, u32[]{:S(2)}) collective-permute-start(bf16[3,128,128]{2,1,0:T(8,128)(2,1)S(1)} %get-tuple-element.8), channel_id=1, source_target_pairs={{0,8},{8,16},{16,24},{24,0},{1,9},{9,17},{17,25},{25,1},{2,10},{10... | collective-permute-start | bytes 294920 | tf_op jit(solution)/shard_map/ppermute | solution.py:256
  51.6 5.6 %collective-permute-start.6 = (bf16[70,3,128]{2,1,0:T(4,128)(2,1)S(1)}, bf16[70,3,128]{2,1,0:T(4,128)(2,1)S(1)}, u32[]{:S(2)}, u32[]{:S(2)}) collective-permute-start(bf16[70,3,128]{2,1,0:T(4,128)(2,1)S(1)} %pad_maximum_fusion.2), channel_id=1, source_target_pairs={{0,1},{1,2},{2,3},{3,4},{4,5},{5,6},{6,7},{8,9},{9,10},{10,11},{11... | collective-permute-start | bytes 161288 | tf_op jit(solution)/shard_map/ppermute | solution.py:256
  55.3 5.7 %collective-permute-start.7 = (bf16[70,3,128]{2,1,0:T(4,128)(2,1)S(1)}, bf16[70,3,128]{2,1,0:T(4,128)(2,1)S(1)}, u32[]{:S(2)}, u32[]{:S(2)}) collective-permute-start(bf16[70,3,128]{2,1,0:T(4,128)(2,1)S(1)} %pad_maximum_fusion.3), channel_id=1, source_target_pairs={{1,0},{2,1},{3,2},{4,3},{5,4},{6,5},{7,6},{9,8},{10,9},{11,10},{12... | collective-permute-start | bytes 161288 | tf_op jit(solution)/shard_map/ppermute | solution.py:257

commit v2 on v1

v2 whole, which is shorter than its diff:
```python
import functools

import jax
import jax.numpy as jnp
from jax import lax
from jax.experimental import pallas as pl
from jax.experimental.pallas import tpu as pltpu
from jax.sharding import PartitionSpec as P

PHASE_I = 8
PHASE_J = 2
PHASES = PHASE_I * PHASE_J
SEG = 16
STRIPS = 16
LEFT = 8
REACH = 3
RIM = 2 * REACH
LANES = 128
WIDE = 256
CHUNKS = 8


def swap_segments(parts, back=False):
    parts = list(parts)
    lane = lax.broadcasted_iota(jnp.int32, parts[0].shape, 1)
    for dist in (1, 2, 4) if back else (4, 2, 1):
        low_side = (lane // (SEG * dist)) % 2 == 0
        turn = LANES - SEG * dist if back else SEG * dist
        for p in range(8):
            if p & dist:
                continue
            low, high = parts[p], parts[p + dist]
            moved = pltpu.roll(jnp.where(low_side, high, low), turn, 1)
            parts[p] = jnp.where(low_side, low, moved)
            parts[p + dist] = jnp.where(low_side, moved, high)
    return parts


def lane_slot(g, p):
    p1, p2, p4 = p & 1, p >> 1 & 1, p >> 2 & 1
    high = p4 ^ ((g >> 1) & (1 - p2))
    return ((high * 2 + p2 + (g & (1 - p1))) & 3) * 2 + p1


def band_body(conv_ref, band_ref, taps_ref, rows_ref):
    f32 = jnp.float32
    g = pl.program_id(0)

    @pl.when(g == 0)
    def _():
        taps_ref[...] = jnp.zeros(taps_ref.shape, f32)
        taps_ref[7:14, 8:15, :] = conv_ref[...].astype(f32)

        def tap_rows(q, carry):
            for half in range(2):
                parts = []
                for p in range(8):
                    pi, pj = (half * 8 + p) // 2, (half * 8 + p) % 2
                    parts.append(taps_ref[q - pi + 7, pl.ds(8 - pj, 8), :])
                for group, part in enumerate(swap_segments(parts)):
                    rows_ref[group, q, :, half * LANES : (half + 1) * LANES] = part
            return carry

        lax.fori_loop(0, 2 * PHASE_I, tap_rows, 0, unroll=4)

    lane = lax.broadcasted_iota(jnp.int32, (SEG, WIDE), 1)
    own = lax.broadcasted_iota(jnp.int32, (SEG, WIDE), 0) == lane % SEG
    for kb in range(2):
        for p in range(PHASES):
            slot = (p >> 3) * 8 + lane_slot(g, p & 7)
            for ub in range(4):
                r = 2 * ub + (p & 1)
                row = rows_ref[g, kb * PHASE_I + (p >> 1), r : r + 1, :]
                band_ref[0, kb * 4 + ub, pl.ds(pl.multiple_of(slot * SEG, SEG), SEG), :] = jnp.where(
                    own, jnp.broadcast_to(row, (SEG, WIDE)), 0.0
                ).astype(jnp.bfloat16)


def band_call(kernel):
    groups = kernel.shape[2] // SEG
    return pl.pallas_call(
        band_body,
        grid=(groups,),
        out_shape=jax.ShapeDtypeStruct((groups, CHUNKS, WIDE, WIDE), jnp.bfloat16),
        in_specs=[pl.BlockSpec(kernel.shape, lambda g: (0, 0, 0))],
        out_specs=pl.BlockSpec((1, CHUNKS, WIDE, WIDE), lambda g: (g, 0, 0, 0)),
        scratch_shapes=[
            pltpu.VMEM((24, 24, LANES), jnp.float32),
            pltpu.VMEM((groups, 2 * PHASE_I, 8, WIDE), jnp.float32),
        ],
        compiler_params=pltpu.CompilerParams(vmem_limit_bytes=16 << 20),
        cost_estimate=pl.CostEstimate(
            flops=16 << 20, bytes_accessed=groups * CHUNKS * WIDE * WIDE * 2, transcendentals=0
        ),
        name="bands",
    )(kernel)


def blocks_body(
    wet_ref,
    state_ref,
    top_ref,
    bottom_ref,
    west_ref,
    east_ref,
    band_a_ref,
    band_b_ref,
    gain_ref,
    bias_ref,
    inner_ref,
    inner_bias_ref,
    outer_ref,
    outer_bias_ref,
    out_ref,
    first_ref,
    second_ref,
    mask_ref,
    wets_ref,
    bands_ref,
    phased_ref,
    grouped_ref,
    cells_ref,
    branch_ref,
    average_ref,
    center_ref,
    sems,
    *,
    tile,
):
    height, width, channels = state_ref.shape
    groups = channels // SEG
    bf16 = jnp.bfloat16
    f32 = jnp.float32
    steps_a = cells_ref.shape[1] * PHASE_J
    steps_b = width // STRIPS
    blocks_a = grouped_ref.shape[1]
    blocks_b = height // PHASE_I
    tiles_i = height // tile
    tiles_j = width // tile

    copies = [
        pltpu.make_async_copy(src, bands_ref.at[layer], sems.at[layer])
        for layer, src in enumerate((band_a_ref, band_b_ref))
    ]
    for copy in copies:
        copy.start()

    rows = height + 2 * RIM
    first_ref[:, LEFT + width + RIM - 6 :, :] = jnp.zeros(
        (first_ref.shape[0], first_ref.shape[1] - LEFT - width - RIM + 6, channels), f32
    )
    first_ref[rows:] = jnp.zeros((first_ref.shape[0] - rows,) + first_ref.shape[1:], f32)
    first_ref[0:RIM, LEFT : LEFT + width, :] = top_ref[0:RIM].astype(f32)
    first_ref[height + RIM : rows, LEFT : LEFT + width, :] = bottom_ref[0:RIM].astype(f32)
    first_ref[0:rows, LEFT - RIM : LEFT, :] = west_ref[:, 0:RIM, :].astype(f32)
    first_ref[0:rows, LEFT + width : LEFT + width + RIM, :] = east_ref[:, 0:RIM, :].astype(f32)

    def widen(i, carry):
        for tj in range(tiles_j):
            wet = wet_ref[i // tile, tj] > 0
            piece = state_ref[i, tj * tile : (tj + 1) * tile, :].astype(f32)
            first_ref[i + RIM, LEFT + tj * tile : LEFT + (tj + 1) * tile, :] = jnp.where(
                wet, piece, 0.0
            )
        return carry

    lax.fori_loop(0, height, widen, 0, unroll=4)

    mask_ref[...] = jnp.zeros(mask_ref.shape, f32)
    for region in range(tiles_i + 2):
        if region == 0:
            mask_ref[region, LEFT : LEFT + width, :] = top_ref[RIM].astype(f32)
            edge = 0
        elif region == tiles_i + 1:
            mask_ref[region, LEFT : LEFT + width, :] = bottom_ref[RIM].astype(f32)
            edge = rows - 1
        else:
            for tj in range(tiles_j):
                flag = jnp.where(wet_ref[region - 1, tj] > 0, 1.0, 0.0)
                mask_ref[region, LEFT + tj * tile : LEFT + (tj + 1) * tile, :] = jnp.full(
                    (tile, channels), flag, f32
                )
            edge = RIM + (region - 1) * tile
        mask_ref[region, LEFT - REACH : LEFT, :] = jnp.broadcast_to(
            west_ref[edge, RIM : RIM + 1, :].astype(f32), (REACH, channels)
        )
        mask_ref[region, LEFT + width : LEFT + width + REACH, :] = jnp.broadcast_to(
            east_ref[edge, RIM : RIM + 1, :].astype(f32), (REACH, channels)
        )
        for t in range(steps_a):
            wets_ref[region, t] = mask_ref[
                region, pl.ds(LEFT - REACH + t, STRIPS, stride=steps_a), :
            ]

    row = lax.broadcasted_iota(jnp.int32, (WIDE, WIDE), 0)
    col = lax.broadcasted_iota(jnp.int32, (WIDE, WIDE), 1)
    share = jnp.where(row // channels == col // channels, 1.0 / channels, 0.0)
    average_ref[...] = share.astype(bf16)
    center_ref[...] = (jnp.where(row == col, 1.0, 0.0) - share).astype(bf16)

    def layer(index, source_ref, start, blocks, steps):
        pairs = steps // PHASE_J

        def to_phases(blk, carry):
            for u in range(pairs + 3):
                for half in range(2):
                    parts = []
                    for p in range(8):
                        pi, pj = (half * 8 + p) // 2, (half * 8 + p) % 2
                        strip = source_ref[
                            blk * PHASE_I + pi, pl.ds(start + 2 * u + pj, STRIPS, stride=steps), :
                        ]
                        parts.append(strip.astype(bf16))
                    for g, part in enumerate(swap_segments(parts)):
                        phased_ref[g, blk, u, :, half * LANES : (half + 1) * LANES] = part
            return carry

        lax.fori_loop(0, blocks + 1, to_phases, 0)
        copies[index].wait()

        def convolve(g, carry):
            slabs = []
            mats = []
            for kb in range(2):
                for ub in range(4):
                    slab = phased_ref[g, kb : kb + blocks, ub : ub + pairs]
                    slabs.append(slab.reshape(blocks * pairs * STRIPS, WIDE))
                    mats.append(bands_ref[index, g, kb * 4 + ub])
            total = jnp.dot(
                jnp.concatenate(slabs, axis=1),
                jnp.concatenate(mats, axis=0),
                preferred_element_type=f32,
            )
            grouped_ref[g, 0:blocks, 0:pairs] = total.astype(bf16).reshape(
                blocks, pairs, STRIPS, WIDE
            )
            return carry

        lax.fori_loop(0, groups, convolve, 0)

        def mix(blk, carry):
            for v in range(pairs):
                for half in range(2):
                    parts = swap_segments(
                        [
                            grouped_ref[g, blk, v, :, half * LANES : (half + 1) * LANES]
                            for g in range(groups)
                        ],
                        back=True,
                    )
                    for p in range(8):
                        pi, pj = (half * 8 + p) // 2, (half * 8 + p) % 2
                        cells_ref[pi, v, :, pj * channels : (pj + 1) * channels] = parts[p]
            count = PHASE_I * pairs * STRIPS
            conv = cells_ref[:, 0:pairs].reshape(count, 2 * channels)
            centered = jnp.dot(conv, center_ref[...], preferred_element_type=f32)
            var = jnp.dot(
                (centered * centered).astype(bf16), average_ref[...], preferred_element_type=f32
            )
            normed = (
                centered * lax.rsqrt(var + 1e-06) * gain_ref[index : index + 1]
                + bias_ref[index : index + 1]
            ).astype(bf16)
            for pj in range(PHASE_J):
                pre = (
                    jnp.dot(
                        normed[:, pj * channels : (pj + 1) * channels],
                        inner_ref[index],
                        preferred_element_type=f32,
                    )
                    + inner_bias_ref[index : index + 1]
                )
                hidden = (pre * (0.5 + 0.5 * lax.erf(pre * 0.7071067811865476))).astype(bf16)
                branch = (
                    jnp.dot(hidden, outer_ref[index], preferred_element_type=f32)
                    + outer_bias_ref[index : index + 1]
                )
                branch = branch.astype(bf16).astype(f32).reshape(
                    PHASE_I, pairs, STRIPS, channels
                )
                for pi in range(PHASE_I):
                    for v in range(pairs):
                        t = 2 * v + pj
                        if index == 0:
                            r = blk * PHASE_I + pi
                            region = jnp.int32(0)
                            for bound in range(REACH, REACH + height + 1, tile):
                                region += (r >= bound).astype(jnp.int32)
                            base = first_ref[
                                r + REACH, pl.ds(LEFT - REACH + t, STRIPS, stride=steps), :
                            ]
                            updated = (base + branch[pi, v]).astype(bf16).astype(f32)
                            second_ref[r, pl.ds(LEFT - REACH + t, STRIPS, stride=steps), :] = (
                                jnp.where(wets_ref[region, t] > 0.0, updated, 0.0)
                            )
                        else:
                            branch_ref[pi, t * STRIPS : (t + 1) * STRIPS, :] = branch[pi, v]
            if index == 1:
                for pi in range(PHASE_I):
                    i = blk * PHASE_I + pi
                    for s in range(0, STRIPS, 2):
                        wet = wet_ref[i // tile, s * steps // tile] > 0
                        delta = jnp.concatenate(
                            [
                                branch_ref[pi, pl.ds(s + k, steps, stride=STRIPS), :]
                                for k in range(2)
                            ],
                            axis=0,
                        )
                        base = second_ref[
                            i + REACH, LEFT + s * steps : LEFT + (s + 2) * steps, :
                        ]
                        out_ref[i, s * steps : (s + 2) * steps, :] = jnp.where(
                            wet, base + delta, 0.0
                        ).astype(bf16)
            return carry

        lax.fori_loop(0, blocks, mix, 0)

    layer(0, first_ref, LEFT - RIM, blocks_a, steps_a)
    layer(1, second_ref, LEFT - REACH, blocks_b, steps_b)


def blocks_call(wet, state, top, bottom, west, east, bands, weights, tile):
    height, width, channels = state.shape
    groups = channels // SEG
    steps_b = width // STRIPS
    blocks_a = pl.cdiv(height + 2 * REACH, PHASE_I)
    steps_a = PHASE_J * pl.cdiv(width + 2 * REACH, STRIPS * PHASE_J)
    pairs_a = steps_a // PHASE_J
    span = LEFT + STRIPS * steps_a
    regions = height // tile + 2
    assert channels == LANES and steps_b == 8 and height % PHASE_I == 0
    vmem = pl.BlockSpec(memory_space=pltpu.VMEM)
    smem = pl.BlockSpec(memory_space=pltpu.SMEM)
    hbm = pl.BlockSpec(memory_space=pl.ANY)
    return pl.pallas_call(
        functools.partial(blocks_body, tile=tile),
        out_shape=jax.ShapeDtypeStruct(state.shape, jnp.bfloat16),
        in_specs=[smem] + [vmem] * 5 + [hbm] * 2 + [vmem] * 6,
        out_specs=vmem,
        scratch_shapes=[
            pltpu.VMEM((PHASE_I * (blocks_a + 1), span, channels), jnp.float32),
            pltpu.VMEM((PHASE_I * blocks_a, span, channels), jnp.float32),
            pltpu.VMEM((regions, span, channels), jnp.float32),
            pltpu.VMEM((regions, steps_a, STRIPS, channels), jnp.float32),
            pltpu.VMEM((2, groups, CHUNKS, WIDE, WIDE), jnp.bfloat16),
            pltpu.VMEM((groups, blocks_a + 1, pairs_a + 3, STRIPS, WIDE), jnp.bfloat16),
            pltpu.VMEM((groups, blocks_a, pairs_a, STRIPS, WIDE), jnp.bfloat16),
            pltpu.VMEM((PHASE_I, pairs_a, STRIPS, 2 * channels), jnp.bfloat16),
            pltpu.VMEM((PHASE_I, width, channels), jnp.float32),
            pltpu.VMEM((WIDE, WIDE), jnp.bfloat16),
            pltpu.VMEM((WIDE, WIDE), jnp.bfloat16),
            pltpu.SemaphoreType.DMA((2,)),
        ],
        compiler_params=pltpu.CompilerParams(vmem_limit_bytes=60 << 20),
        name="blocks",
    )(wet, state, top, bottom, west, east, *bands, *weights)


def shift_pair(head, tail, axis, closed):
    count = lax.axis_size(axis)
    ends = count if closed else count - 1
    before = lax.ppermute(tail, axis, [(i, (i + 1) % count) for i in range(ends)])
    after = lax.ppermute(head, axis, [((i + 1) % count, i) for i in range(ends)])
    return before, after


def per_device(
    ocean_field,
    wet_tiles,
    conv_weight,
    norm_gain,
    norm_bias,
    inner_weight,
    inner_bias,
    outer_weight,
    outer_bias,
):
    height, _, channels = ocean_field.shape
    tile = height // wet_tiles.shape[0]
    dtype = ocean_field.dtype

    def rim_rows(edge, flags):
        wet = jnp.repeat(flags, tile)[None, :, None]
        kept = jnp.where(wet > 0, edge, jnp.zeros((), dtype))
        return jnp.concatenate(
            [kept, jnp.broadcast_to(wet, (1,) + edge.shape[1:]).astype(dtype)], axis=0
        )

    top, bottom = shift_pair(
        rim_rows(ocean_field[:RIM], wet_tiles[0]),
        rim_rows(ocean_field[-RIM:], wet_tiles[-1]),
        "lon",
        True,
    )

    def rim_cols(edge, flags, above, below):
        wet = jnp.repeat(flags, tile)[:, None, None]
        kept = jnp.where(wet > 0, edge, jnp.zeros((), dtype))
        middle = jnp.concatenate(
            [kept, jnp.broadcast_to(wet, (height, 1, channels)).astype(dtype)], axis=1
        )
        ends = [
            jnp.concatenate(
                [rim[:RIM], jnp.broadcast_to(rim[RIM:, :1], (RIM, 1, channels))], axis=1
            )
            for rim in (above, below)
        ]
        return jnp.concatenate([ends[0], middle, ends[1]], axis=0)

    west, east = shift_pair(
        rim_cols(ocean_field[:, :RIM], wet_tiles[:, 0], top[:, :RIM], bottom[:, :RIM]),
        rim_cols(ocean_field[:, -RIM:], wet_tiles[:, -1], top[:, -RIM:], bottom[:, -RIM:]),
        "lat",
        False,
    )
    bands = [band_call(conv_weight[layer]) for layer in range(conv_weight.shape[0])]
    weights = (
        jnp.tile(norm_gain, (1, 2)),
        jnp.tile(norm_bias, (1, 2)),
        inner_weight,
        inner_bias,
        outer_weight,
        outer_bias,
    )
    return blocks_call(wet_tiles, ocean_field, top, bottom, west, east, bands, weights, tile)


def solution(mesh):
    return jax.shard_map(
        per_device,
        mesh=mesh,
        in_specs=(P("lon", "lat", None), P("lon", "lat"), P(), P(), P(), P(), P(), P(), P()),
        out_specs=P("lon", "lat", None),
        check_vma=False,
    )
```

time: 87.1 us -> 80 us (0.918)
  waiting for transfers between devices: 15.5 us -> 4.04 us
  local copies, waits for them, and re-layouts: 0.47 us -> 11 us
  starting transfers between devices: 17.2 us -> 9.01 us
  between operations: 0.29 us -> 2.77 us
  Pallas kernels: 50.6 us -> 49.2 us
    ppermute x4 -> x2, waiting for transfers between devices: 11.9 us -> 4.04 us  [shift_pair(): lax.ppermute(head, axis, [((i + 1) % count, i) for i in range(ends)])]
    unnamed x20 -> x16, local copies, waits for them, and re-layouts: 0.06 us -> 7.81 us
    ppermute x4 -> x2, starting transfers between devices: 9.45 us -> 4.05 us  [shift_pair(): lax.ppermute(tail, axis, [(i, (i + 1) % count) for i in range(ends)])]
    ppermute x4 -> x2, waiting for transfers between devices: 3.61 us -> 0.01 us  [shift_pair(): lax.ppermute(tail, axis, [(i, (i + 1) % count) for i in range(ends)])]
    ppermute x4 -> x2, starting transfers between devices: 7.72 us -> 4.96 us  [shift_pair(): lax.ppermute(head, axis, [((i + 1) % count, i) for i in range(ends)])]
    pallas_call x2 -> x3, Pallas kernels: 50.6 us -> 49.2 us  [the longest x1 44.9 us: blocks_call(): pl.pallas_call(functools.partial(blocks_body, tile=tile), out_shape=jax.S...]
    slice x10 -> x3, local copies, waits for them, and re-layouts: 0.18 us -> 1.34 us  [the longest x1 1.32 us: per_device(): wet_tiles[:, 0]]
    select_n x1 -> x2, other arithmetic: 1.95 us -> 2.14 us  [the longest x1 1.12 us: rim_rows(): kept = jnp.where(wet > 0, edge, jnp.zeros((), dtype))]
  transfers between devices with their start and end apart: 8 -> 4, of which waited for: 6 -> 1; matrix products, arithmetic and copies ran while one was open for 0% -> 6% of each run, Pallas kernels for 0% -> 5%
where the time goes in v2:
time: 80 us; the launch traced here: 79.6 us
  Pallas kernels  49.2 us (62%)
  local copies, waits for them, and re-layouts  11 us (14%)
  starting transfers between devices  9.01 us (11%)
  waiting for transfers between devices  4.04 us (5%)
  other arithmetic  3.6 us (4%)
  between operations  2.77 us (3%)
    pallas_call x1, Pallas kernels, blocks_call(): pl.pallas_call(functools.partial(blocks_body, tile=tile), out_shape=jax.S...  44.9 us
    unnamed x16, local copies, waits for them, and re-layouts  7.81 us
    ppermute x2, starting transfers between devices, shift_pair(): lax.ppermute(head, axis, [((i + 1) % count, i) for i in range(ends)])  4.96 us
    pallas_call x2, Pallas kernels, band_call(): pl.pallas_call(band_body, grid=(groups,), out_shape=jax.ShapeDtypeStruct(...  4.26 us
    ppermute x2, starting transfers between devices, shift_pair(): lax.ppermute(tail, axis, [(i, (i + 1) % count) for i in range(ends)])  4.05 us
    ppermute x2, waiting for transfers between devices, shift_pair(): lax.ppermute(head, axis, [((i + 1) % count, i) for i in range(ends)])  4.04 us
  transfers between devices with their start and end apart: 4, of which 1 were waited for; matrix products, arithmetic and copies ran while one was open for 6% of the time, Pallas kernels for 5%

profile of v2, /device:TPU:1, one launch (start us, length us, event | category | flops | bytes accessed | tf_op | source)
XLA Modules:
  0.0 79.6 jit_solution(17219370350173804164)
XLA Ops:
  0.0 0.0 copy-start
  0.0 0.7 convert_bitcast_fusion
  0.7 0.7 compare_bitcast_fusion
  1.3 0.1 broadcast_in_dim.87
  1.4 0.1 convert_element_type.37
  1.5 0.1 broadcast_in_dim.84
  1.6 0.1 gt.32
  1.7 1.1 %slice_select_fusion = (bf16[6,128,128]{2,1,0:T(8,128)(2,1)S(1)}, bf16[6,128,128]{2,1,0:T(8,128)(2,1)S(1)}) fusion(bf16[64,128,128]{2,1,0:T(8,128)(2,1)} %state_ref.1, pred[128]{0:T(512)(128)(4,1)S(1)} %gt.32), kind=kLoop, calls=%fused_computation.7 | loop fusion | flops 196608 | bytes 786560 | tf_op jit(solution)/shard_map/jit(_where)/select_n | solution.py:386
  2.8 0.1 broadcast_in_dim.88
  2.9 3.0 %collective-permute-start.1 = (bf16[7,128,128]{2,1,0:T(8,128)(2,1)S(1)}, bf16[7,128,128]{2,1,0:T(8,128)(2,1)S(1)}, u32[]{:S(2)}, u32[]{:S(2)}) collective-permute-start(bf16[7,128,128]{2,1,0:T(8,128)(2,1)S(1)} %get-tuple-element.17), channel_id=1, source_target_pairs={{8,0},{16,8},{24,16},{0,24},{9,1},{17,9},{25,17},{1,25},{10,2},{18... | collective-permute-start | bytes 688136 | tf_op jit(solution)/shard_map/ppermute | solution.py:365
  6.0 0.0 collective-permute-start
  6.0 1.3 %fusion.10 = (s32[1,1]{1,0:T(1,128)}, s32[1,1]{1,0:T(1,128)}) fusion(s32[1,2]{1,0:T(1,128)} %wet_ref.1), kind=kLoop, calls=%fused_computation.30 | loop fusion | bytes 16 | tf_op jit(solution)/shard_map/slice | solution.py:413
  9.8 0.0 copy-done
  9.9 0.7 broadcast_bitcast_fusion
  10.5 0.9 %fusion.9 = (bf16[1,7,7,128]{3,0,2,1:T(2,128)(2,1)S(1)}, bf16[1,7,7,128]{3,0,2,1:T(2,128)(2,1)S(1)}) fusion(bf16[2,7,7,128]{3,0,2,1:T(2,128)(2,1)} %param.11), kind=kLoop, calls=%fused_computation.29 | loop fusion | bytes 50176 | tf_op jit(solution)/shard_map/slice | solution.py:418
  11.4 2.1 %bands.3.band_b_ref = bf16[8,8,256,256]{3,2,1,0:T(8,128)(2,1)S(1)} custom-call(bf16[7,7,128]{2,1,0:T(8,128)(2,1)S(1)} %get-tuple-element.23.conv_ref), custom_call_target="tpu_custom_call" | custom-call | flops 16777216 | bytes 8388608 | tf_op jit(solution)/shard_map/bands/pallas_call | solution.py:81
  13.6 0.0 copy-start.1
  13.6 3.2 %copy-done.1 = bf16[8,8,256,256]{3,2,1,0:T(8,128)(2,1)} copy-done((bf16[8,8,256,256]{3,2,1,0:T(8,128)(2,1)}, bf16[8,8,256,256]{3,2,1,0:T(8,128)(2,1)S(1)}, u32[]{:S(2)}) %copy-start.1) | copy-done | bytes 8388632
  16.8 2.1 %bands.2.band_a_ref = bf16[8,8,256,256]{3,2,1,0:T(8,128)(2,1)S(1)} custom-call(bf16[7,7,128]{2,1,0:T(8,128)(2,1)S(1)} %get-tuple-element.24.conv_ref), custom_call_target="tpu_custom_call" | custom-call | flops 16777216 | bytes 8388608 | tf_op jit(solution)/shard_map/bands/pallas_call | solution.py:81
  18.9 0.0 copy-start.2
  18.9 3.2 %copy-done.2 = bf16[8,8,256,256]{3,2,1,0:T(8,128)(2,1)} copy-done((bf16[8,8,256,256]{3,2,1,0:T(8,128)(2,1)}, bf16[8,8,256,256]{3,2,1,0:T(8,128)(2,1)S(1)}, u32[]{:S(2)}) %copy-start.2) | copy-done | bytes 8388632
  22.2 1.0 %slice_select_fusion.2 = (bf16[64,6,128]{2,1,0:T(8,128)(2,1)S(1)}, bf16[64,6,128]{2,1,0:T(8,128)(2,1)S(1)}) fusion(bf16[64,128,128]{2,1,0:T(8,128)(2,1)} %state_ref.1, pred[]{:T(512)} %bitcast.7, pred[]{:T(512)} %bitcast.3), kind=kLoop, calls=%fused_computation.13 | loop fusion | flops 98304 | bytes 393218 | tf_op jit(solution)/shard_map/jit(_where)/select_n | solution.py:400
  23.2 0.0 collective-permute-done.1.bottom_ref
  23.2 0.0 copy-start.3
  23.2 0.0 collective-permute-done.top_ref
  23.4 4.0 %collective-permute-start.2 = (bf16[76,7,128]{2,1,0:T(8,128)(2,1)S(1)}, bf16[76,7,128]{2,1,0:T(8,128)(2,1)S(1)}, u32[]{:S(2)}, u32[]{:S(2)}) collective-permute-start(bf16[76,7,128]{2,1,0:T(8,128)(2,1)S(1)} %fusion.4), channel_id=1, source_target_pairs={{0,1},{1,2},{2,3},{3,4},{4,5},{5,6},{6,7},{8,9},{9,10},{10,11},{11... | collective-permute-start | bytes 408584 | tf_op jit(solution)/shard_map/ppermute | solution.py:364
  27.5 1.9 %collective-permute-start.3 = (bf16[76,7,128]{2,1,0:T(8,128)(2,1)S(1)}, bf16[76,7,128]{2,1,0:T(8,128)(2,1)S(1)}, u32[]{:S(2)}, u32[]{:S(2)}) collective-permute-start(bf16[76,7,128]{2,1,0:T(8,128)(2,1)S(1)} %fusion.6), channel_id=1, source_target_pairs={{1,0},{2,1},{3,2},{4,3},{5,4},{6,5},{7,6},{9,8},{10,9},{11,10},{12... | collective-permute-start | bytes 408584 | tf_op jit(solution)/shard_map/ppermute | solution.py:365
  29.4 0.6 copy_bitcast_fusion.2
  30.0 0.0 collective-permute-done.2.west_ref
  30.0 4.0 %collective-permute-done.3.east_ref = bf16[76,7,128]{2,1,0:T(8,128)(2,1)S(1)} collective-permute-done((bf16[76,7,128]{2,1,0:T(8,128)(2,1)S(1)}, bf16[76,7,128]{2,1,0:T(8,128)(2,1)S(1)}, u32[]{:S(2)}, u32[]{:S(2)}) %collective-permute-start.3) | collective-permute-done | bytes 136224 | tf_op jit(solution)/shard_map/ppermute | solution.py:365
  34.1 0.7 copy-done.6
  34.7 44.9 %blocks.1 = bf16[64,128,128]{2,1,0:T(8,128)(2,1)} custom-call(s32[1,2]{1,0:T(1,128)} %wet_ref.1, bf16[64,128,128]{2,1,0:T(8,128)(2,1)} %state_ref.1, bf16[7,128,128]{2,1,0:T(8,128)(2,1)} %copy-done.4, bf16[7,128,128]{2,1,0:T(8,128)(2,1)} %copy-done.3, bf16[76,7,128]{2,1,0:T(8,128)(2,1)} %copy-done.5, bf16[76,7,128]{2,1,0:T(8,128)(2,1)} %copy-done.6, ...), custom_call_target="tpu_custom_call" | custom-call | tf_op jit(solution)/shard_map/blocks/pallas_call | solution.py:337
  (19 shorter events, 0.2 us)
Async XLA Ops:
  0.0 9.8 %copy-start = (f32[2,128]{1,0:T(2,128)S(1)}, f32[2,128]{1,0:T(2,128)}, u32[]{:S(2)}) copy-start(f32[2,128]{1,0:T(2,128)} %param.12) | copy-start | bytes 3076
  2.9 20.3 %collective-permute-start.1 = (bf16[7,128,128]{2,1,0:T(8,128)(2,1)S(1)}, bf16[7,128,128]{2,1,0:T(8,128)(2,1)S(1)}, u32[]{:S(2)}, u32[]{:S(2)}) collective-permute-start(bf16[7,128,128]{2,1,0:T(8,128)(2,1)S(1)} %get-tuple-element.17), channel_id=1, source_target_pairs={{8,0},{16,8},{24,16},{0,24},{9,1},{17,9},{25,17},{1,25},{10,2},{18... | collective-permute-start | bytes 688136 | tf_op jit(solution)/shard_map/ppermute | solution.py:365
  6.0 17.3 %collective-permute-start = (bf16[7,128,128]{2,1,0:T(8,128)(2,1)S(1)}, bf16[7,128,128]{2,1,0:T(8,128)(2,1)S(1)}, u32[]{:S(2)}, u32[]{:S(2)}) collective-permute-start(bf16[7,128,128]{2,1,0:T(8,128)(2,1)S(1)} %get-tuple-element.18), channel_id=1, source_target_pairs={{0,8},{8,16},{16,24},{24,0},{1,9},{9,17},{17,25},{25,1},{2,10},{10... | collective-permute-start | bytes 688136 | tf_op jit(solution)/shard_map/ppermute | solution.py:364
  13.6 3.2 %copy-start.1 = (bf16[8,8,256,256]{3,2,1,0:T(8,128)(2,1)}, bf16[8,8,256,256]{3,2,1,0:T(8,128)(2,1)S(1)}, u32[]{:S(2)}) copy-start(bf16[8,8,256,256]{3,2,1,0:T(8,128)(2,1)S(1)} %bands.3.band_b_ref) | copy-start | bytes 25165828
  18.9 3.2 %copy-start.2 = (bf16[8,8,256,256]{3,2,1,0:T(8,128)(2,1)}, bf16[8,8,256,256]{3,2,1,0:T(8,128)(2,1)S(1)}, u32[]{:S(2)}) copy-start(bf16[8,8,256,256]{3,2,1,0:T(8,128)(2,1)S(1)} %bands.2.band_a_ref) | copy-start | bytes 25165828
  23.2 10.9 %copy-start.3 = (bf16[7,128,128]{2,1,0:T(8,128)(2,1)}, bf16[7,128,128]{2,1,0:T(8,128)(2,1)S(1)}, u32[]{:S(2)}) copy-start(bf16[7,128,128]{2,1,0:T(8,128)(2,1)S(1)} %collective-permute-done.1.bottom_ref) | copy-start | bytes 688132
  23.3 10.8 %copy-start.4 = (bf16[7,128,128]{2,1,0:T(8,128)(2,1)}, bf16[7,128,128]{2,1,0:T(8,128)(2,1)S(1)}, u32[]{:S(2)}) copy-start(bf16[7,128,128]{2,1,0:T(8,128)(2,1)S(1)} %collective-permute-done.top_ref) | copy-start | bytes 688132
  23.4 6.6 %collective-permute-start.2 = (bf16[76,7,128]{2,1,0:T(8,128)(2,1)S(1)}, bf16[76,7,128]{2,1,0:T(8,128)(2,1)S(1)}, u32[]{:S(2)}, u32[]{:S(2)}) collective-permute-start(bf16[76,7,128]{2,1,0:T(8,128)(2,1)S(1)} %fusion.4), channel_id=1, source_target_pairs={{0,1},{1,2},{2,3},{3,4},{4,5},{5,6},{6,7},{8,9},{9,10},{10,11},{11... | collective-permute-start | bytes 408584 | tf_op jit(solution)/shard_map/ppermute | solution.py:364
  27.5 6.5 %collective-permute-start.3 = (bf16[76,7,128]{2,1,0:T(8,128)(2,1)S(1)}, bf16[76,7,128]{2,1,0:T(8,128)(2,1)S(1)}, u32[]{:S(2)}, u32[]{:S(2)}) collective-permute-start(bf16[76,7,128]{2,1,0:T(8,128)(2,1)S(1)} %fusion.6), channel_id=1, source_target_pairs={{1,0},{2,1},{3,2},{4,3},{5,4},{6,5},{7,6},{9,8},{10,9},{11,10},{12... | collective-permute-start | bytes 408584 | tf_op jit(solution)/shard_map/ppermute | solution.py:365
  30.0 4.0 %copy-start.5 = (bf16[76,7,128]{2,1,0:T(8,128)(2,1)}, bf16[76,7,128]{2,1,0:T(8,128)(2,1)S(1)}, u32[]{:S(2)}) copy-start(bf16[76,7,128]{2,1,0:T(8,128)(2,1)S(1)} %collective-permute-done.2.west_ref) | copy-start | bytes 408580
  34.1 0.7 copy-start.6

commit v3 on v2

--- a/solution.py
+++ b/solution.py
@@ -58,42 +58,126 @@
                     pi, pj = (half * 8 + p) // 2, (half * 8 + p) % 2
                     parts.append(taps_ref[q - pi + 7, pl.ds(8 - pj, 8), :])
                 for group, part in enumerate(swap_segments(parts)):
-                    rows_ref[group, q, :, half * LANES : (half + 1) * LANES] = part
+                    rows_ref[group, q, half] = part
             return carry
 
         lax.fori_loop(0, 2 * PHASE_I, tap_rows, 0, unroll=4)
 
-    lane = lax.broadcasted_iota(jnp.int32, (SEG, WIDE), 1)
-    own = lax.broadcasted_iota(jnp.int32, (SEG, WIDE), 0) == lane % SEG
+    lane = lax.broadcasted_iota(jnp.int32, (SEG, LANES), 1)
+    own = lax.broadcasted_iota(jnp.int32, (SEG, LANES), 0) == lane % SEG
     for kb in range(2):
         for p in range(PHASES):
             slot = (p >> 3) * 8 + lane_slot(g, p & 7)
+            at = pl.ds(pl.multiple_of(slot * SEG, SEG), SEG)
             for ub in range(4):
                 r = 2 * ub + (p & 1)
-                row = rows_ref[g, kb * PHASE_I + (p >> 1), r : r + 1, :]
-                band_ref[0, kb * 4 + ub, pl.ds(pl.multiple_of(slot * SEG, SEG), SEG), :] = jnp.where(
-                    own, jnp.broadcast_to(row, (SEG, WIDE)), 0.0
-                ).astype(jnp.bfloat16)
-
-
-def band_call(kernel):
-    groups = kernel.shape[2] // SEG
+                for half in range(2):
+                    row = rows_ref[g, kb * PHASE_I + (p >> 1), half, r : r + 1, :]
+                    band_ref[0, kb * 4 + ub, half, at, :] = jnp.where(
+                        own, jnp.broadcast_to(row, (SEG, LANES)), 0.0
+                    ).astype(jnp.bfloat16)
+
+
+def band_call(kernels, layer):
+    groups = kernels.shape[3] // SEG
     return pl.pallas_call(
         band_body,
         grid=(groups,),
-        out_shape=jax.ShapeDtypeStruct((groups, CHUNKS, WIDE, WIDE), jnp.bfloat16),
-        in_specs=[pl.BlockSpec(kernel.shape, lambda g: (0, 0, 0))],
-        out_specs=pl.BlockSpec((1, CHUNKS, WIDE, WIDE), lambda g: (g, 0, 0, 0)),
+        out_shape=jax.ShapeDtypeStruct((groups, CHUNKS, 2, WIDE, LANES), jnp.bfloat16),
+        in_specs=[pl.BlockSpec((None,) + kernels.shape[1:], lambda g: (layer, 0, 0, 0))],
+        out_specs=pl.BlockSpec((1, CHUNKS, 2, WIDE, LANES), lambda g: (g, 0, 0, 0, 0)),
         scratch_shapes=[
             pltpu.VMEM((24, 24, LANES), jnp.float32),
-            pltpu.VMEM((groups, 2 * PHASE_I, 8, WIDE), jnp.float32),
+            pltpu.VMEM((groups, 2 * PHASE_I, 2, 8, LANES), jnp.float32),
         ],
         compiler_params=pltpu.CompilerParams(vmem_limit_bytes=16 << 20),
         cost_estimate=pl.CostEstimate(
             flops=16 << 20, bytes_accessed=groups * CHUNKS * WIDE * WIDE * 2, transcendentals=0
         ),
         name="bands",
-    )(kernel)
+    )(kernels)
+
+
+def rim_rows_body(wet_ref, upper_ref, lower_ref, head_ref, tail_ref, *, tile):
+    for rows_ref, out_ref, ti in ((upper_ref, head_ref, 0), (lower_ref, tail_ref, wet_ref.shape[0] - 1)):
+        height, width, channels = rows_ref.shape
+        first = 0 if ti == 0 and rows_ref is upper_ref else height - RIM
+        for tj in range(width // tile):
+            wet = wet_ref[ti, tj] > 0
+            at = slice(tj * tile, (tj + 1) * tile)
+            for r in range(RIM):
+                out_ref[r, at, :] = jnp.where(
+                    wet, rows_ref[first + r, at, :].astype(jnp.float32), 0.0
+                ).astype(jnp.bfloat16)
+            out_ref[RIM, at, :] = jnp.full(
+                (tile, channels), jnp.where(wet, 1.0, 0.0), jnp.float32
+            ).astype(jnp.bfloat16)
+
+
+def rim_rows_call(wet, state, tile):
+    height, width, channels = state.shape
+    shape = jax.ShapeDtypeStruct((RIM + 1, width, channels), jnp.bfloat16)
+    last = height // 8 - 1
+    return pl.pallas_call(
+        functools.partial(rim_rows_body, tile=tile),
+        grid=(1,),
+        out_shape=[shape, shape],
+        in_specs=[
+            pl.BlockSpec(memory_space=pltpu.SMEM),
+            pl.BlockSpec((8, width, channels), lambda i: (0, 0, 0)),
+            pl.BlockSpec((8, width, channels), lambda i: (last, 0, 0)),
+        ],
+        out_specs=[pl.BlockSpec(shape.shape, lambda i: (0, 0, 0))] * 2,
+        compiler_params=pltpu.CompilerParams(vmem_limit_bytes=8 << 20),
+        name="rim_rows",
+    )(wet, state, state)
+
+
+def rim_cols_body(wet_ref, left_ref, right_ref, top_ref, bottom_ref, head_ref, tail_ref, *, tile):
+    f32 = jnp.float32
+    bf16 = jnp.bfloat16
+    height, chunk, channels = left_ref.shape
+    width = top_ref.shape[1]
+    tiles_i, tiles_j = wet_ref.shape
+    for cols_ref, out_ref, tj, first, side in (
+        (left_ref, head_ref, 0, 0, 0),
+        (right_ref, tail_ref, tiles_j - 1, chunk - RIM, width - RIM),
+    ):
+        for ti in range(tiles_i):
+            wet = wet_ref[ti, tj] > 0
+            at = slice(RIM + ti * tile, RIM + (ti + 1) * tile)
+            piece = cols_ref[ti * tile : (ti + 1) * tile].astype(f32)
+            kept = jnp.where(wet, piece[:, first : first + RIM], 0.0)
+            flag = jnp.full((tile, 1, channels), jnp.where(wet, 1.0, 0.0), f32)
+            out_ref[at] = jnp.concatenate([kept, flag], axis=1).astype(bf16)
+        for rim_ref, at in ((top_ref, 0), (bottom_ref, height + RIM)):
+            kept = rim_ref[0:RIM, side : side + RIM, :].astype(f32)
+            flag = rim_ref[RIM : RIM + 1, side : side + 1, :].astype(f32)
+            out_ref[at : at + RIM] = jnp.concatenate(
+                [kept, jnp.broadcast_to(flag, (RIM, 1, channels))], axis=1
+            ).astype(bf16)
+
+
+def rim_cols_call(wet, state, top, bottom, tile):
+    height, width, channels = state.shape
+    shape = jax.ShapeDtypeStruct((height + 2 * RIM, RIM + 1, channels), jnp.bfloat16)
+    last = width // 8 - 1
+    whole = pl.BlockSpec(top.shape, lambda i: (0, 0, 0))
+    return pl.pallas_call(
+        functools.partial(rim_cols_body, tile=tile),
+        grid=(1,),
+        out_shape=[shape, shape],
+        in_specs=[
+            pl.BlockSpec(memory_space=pltpu.SMEM),
+            pl.BlockSpec((height, 8, channels), lambda i: (0, 0, 0)),
+            pl.BlockSpec((height, 8, channels), lambda i: (0, last, 0)),
+            whole,
+            whole,
+        ],
+        out_specs=[pl.BlockSpec(shape.shape, lambda i: (0, 0, 0))] * 2,
+        compiler_params=pltpu.CompilerParams(vmem_limit_bytes=8 << 20),
+        name="rim_cols",
+    )(wet, state, state, top, bottom)
 
 
 def blocks_body(
@@ -116,14 +200,14 @@
     second_ref,
     mask_ref,
     wets_ref,
-    bands_ref,
     phased_ref,
     grouped_ref,
     cells_ref,
     branch_ref,
     average_ref,
     center_ref,
-    sems,
+    inner_wide_ref,
+    outer_half_ref,
     *,
     tile,
 ):
@@ -131,19 +215,12 @@
     groups = channels // SEG
     bf16 = jnp.bfloat16
     f32 = jnp.float32
-    steps_a = cells_ref.shape[1] * PHASE_J
+    steps_a = cells_ref.shape[2] * PHASE_J
     steps_b = width // STRIPS
-    blocks_a = grouped_ref.shape[1]
+    blocks_a = grouped_ref.shape[2]
     blocks_b = height // PHASE_I
     tiles_i = height // tile
     tiles_j = width // tile
-
-    copies = [
-        pltpu.make_async_copy(src, bands_ref.at[layer], sems.at[layer])
-        for layer, src in enumerate((band_a_ref, band_b_ref))
-    ]
-    for copy in copies:
-        copy.start()
 
     rows = height + 2 * RIM
     first_ref[:, LEFT + width + RIM - 6 :, :] = jnp.zeros(
@@ -198,8 +275,28 @@
     average_ref[...] = share.astype(bf16)
     center_ref[...] = (jnp.where(row == col, 1.0, 0.0) - share).astype(bf16)
 
-    def layer(index, source_ref, start, blocks, steps):
+    for index in range(2):
+        hidden_dim = inner_ref.shape[2]
+        inner_wide_ref[index, 0:channels, :] = inner_ref[index]
+        rest = inner_bias_ref[index : index + 1]
+        parts = []
+        for _ in range(3):
+            parts.append(rest.astype(bf16).astype(f32))
+            rest = rest - parts[-1]
+        which = lax.broadcasted_iota(jnp.int32, (channels, hidden_dim), 0)
+        tail = jnp.zeros((channels, hidden_dim), f32)
+        for k, part in enumerate(parts):
+            tail = jnp.where(which == k, part, tail)
+        inner_wide_ref[index, channels : 2 * channels, :] = tail.astype(bf16)
+        outer_half_ref[index] = (outer_ref[index].astype(f32) * 0.5).astype(bf16)
+
+    def layer(index, source_ref, band_ref, start, blocks, steps):
         pairs = steps // PHASE_J
+        gain = jnp.concatenate([gain_ref[index : index + 1]] * 2, axis=1)
+        shift = jnp.concatenate([bias_ref[index : index + 1]] * 2, axis=1)
+        bias_lanes = jnp.where(
+            lax.broadcasted_iota(jnp.int32, (PHASE_I * pairs * STRIPS, channels), 1) < 3, 1.0, 0.0
+        ).astype(bf16)
 
         def to_phases(blk, carry):
             for u in range(pairs + 3):
@@ -212,28 +309,30 @@
                         ]
                         parts.append(strip.astype(bf16))
                     for g, part in enumerate(swap_segments(parts)):
-                        phased_ref[g, blk, u, :, half * LANES : (half + 1) * LANES] = part
+                        phased_ref[g, half, blk, u] = part
             return carry
 
         lax.fori_loop(0, blocks + 1, to_phases, 0)
-        copies[index].wait()
 
         def convolve(g, carry):
             slabs = []
             mats = []
             for kb in range(2):
                 for ub in range(4):
-                    slab = phased_ref[g, kb : kb + blocks, ub : ub + pairs]
-                    slabs.append(slab.reshape(blocks * pairs * STRIPS, WIDE))
-                    mats.append(bands_ref[index, g, kb * 4 + ub])
+                    for half in range(2):
+                        slab = phased_ref[g, half, kb : kb + blocks, ub : ub + pairs]
+                        slabs.append(slab.reshape(blocks * pairs * STRIPS, LANES))
+                    band = band_ref.at[g, kb * 4 + ub]
+                    mats.append(jnp.concatenate([band[0], band[1]], axis=1))
             total = jnp.dot(
                 jnp.concatenate(slabs, axis=1),
                 jnp.concatenate(mats, axis=0),
                 preferred_element_type=f32,
-            )
-            grouped_ref[g, 0:blocks, 0:pairs] = total.astype(bf16).reshape(
-                blocks, pairs, STRIPS, WIDE
-            )
+            ).astype(bf16)
+            for half in range(2):
+                grouped_ref[g, half, 0:blocks, 0:pairs] = total[
+                    :, half * LANES : (half + 1) * LANES
+                ].reshape(blocks, pairs, STRIPS, LANES)
             return carry
 
         lax.fori_loop(0, groups, convolve, 0)
@@ -242,42 +341,37 @@
             for v in range(pairs):
                 for half in range(2):
                     parts = swap_segments(
-                        [
-                            grouped_ref[g, blk, v, :, half * LANES : (half + 1) * LANES]
-                            for g in range(groups)
-                        ],
-                        back=True,
+                        [grouped_ref[g, half, blk, v] for g in range(groups)], back=True
                     )
                     for p in range(8):
                         pi, pj = (half * 8 + p) // 2, (half * 8 + p) % 2
-                        cells_ref[pi, v, :, pj * channels : (pj + 1) * channels] = parts[p]
+                        cells_ref[pj, pi, v] = parts[p]
             count = PHASE_I * pairs * STRIPS
-            conv = cells_ref[:, 0:pairs].reshape(count, 2 * channels)
+            conv = jnp.concatenate(
+                [cells_ref[pj, :, 0:pairs].reshape(count, channels) for pj in range(PHASE_J)],
+                axis=1,
+            )
             centered = jnp.dot(conv, center_ref[...], preferred_element_type=f32)
             var = jnp.dot(
                 (centered * centered).astype(bf16), average_ref[...], preferred_element_type=f32
             )
             normed = (
-                centered * lax.rsqrt(var + 1e-06) * gain_ref[index : index + 1]
-                + bias_ref[index : index + 1]
+                centered * lax.rsqrt(var + 1e-06) * gain
+                + shift
             ).astype(bf16)
             for pj in range(PHASE_J):
-                pre = (
-                    jnp.dot(
-                        normed[:, pj * channels : (pj + 1) * channels],
-                        inner_ref[index],
-                        preferred_element_type=f32,
-                    )
-                    + inner_bias_ref[index : index + 1]
+                pre = jnp.dot(
+                    jnp.concatenate(
+                        [normed[:, pj * channels : (pj + 1) * channels], bias_lanes], axis=1
+                    ),
+                    inner_wide_ref[index],
+                    preferred_element_type=f32,
                 )
-                hidden = (pre * (0.5 + 0.5 * lax.erf(pre * 0.7071067811865476))).astype(bf16)
+                hidden = (pre * (1.0 + lax.erf(pre * 0.7071067811865476))).astype(bf16)
                 branch = (
-                    jnp.dot(hidden, outer_ref[index], preferred_element_type=f32)
+                    jnp.dot(hidden, outer_half_ref[index], preferred_element_type=f32)
                     + outer_bias_ref[index : index + 1]
-                )
-                branch = branch.astype(bf16).astype(f32).reshape(
-                    PHASE_I, pairs, STRIPS, channels
-                )
+                ).reshape(PHASE_I, pairs, STRIPS, channels)
                 for pi in range(PHASE_I):
                     for v in range(pairs):
                         t = 2 * v + pj
@@ -289,10 +383,9 @@
                             base = first_ref[
                                 r + REACH, pl.ds(LEFT - REACH + t, STRIPS, stride=steps), :
                             ]
-                            updated = (base + branch[pi, v]).astype(bf16).astype(f32)
                             second_ref[r, pl.ds(LEFT - REACH + t, STRIPS, stride=steps), :] = (
-                                jnp.where(wets_ref[region, t] > 0.0, updated, 0.0)
-                            )
+                                base + branch[pi, v]
+                            ) * wets_ref[region, t]
                         else:
                             branch_ref[pi, t * STRIPS : (t + 1) * STRIPS, :] = branch[pi, v]
             if index == 1:
@@ -317,8 +410,8 @@
 
         lax.fori_loop(0, blocks, mix, 0)
 
-    layer(0, first_ref, LEFT - RIM, blocks_a, steps_a)
-    layer(1, second_ref, LEFT - REACH, blocks_b, steps_b)
+    layer(0, first_ref, band_a_ref, LEFT - RIM, blocks_a, steps_a)
+    layer(1, second_ref, band_b_ref, LEFT - REACH, blocks_b, steps_b)
 
 
 def blocks_call(wet, state, top, bottom, west, east, bands, weights, tile):
@@ -333,27 +426,26 @@
     assert channels == LANES and steps_b == 8 and height % PHASE_I == 0
     vmem = pl.BlockSpec(memory_space=pltpu.VMEM)
     smem = pl.BlockSpec(memory_space=pltpu.SMEM)
-    hbm = pl.BlockSpec(memory_space=pl.ANY)
     return pl.pallas_call(
         functools.partial(blocks_body, tile=tile),
         out_shape=jax.ShapeDtypeStruct(state.shape, jnp.bfloat16),
-        in_specs=[smem] + [vmem] * 5 + [hbm] * 2 + [vmem] * 6,
+        in_specs=[smem] + [vmem] * 13,
         out_specs=vmem,
         scratch_shapes=[
             pltpu.VMEM((PHASE_I * (blocks_a + 1), span, channels), jnp.float32),
             pltpu.VMEM((PHASE_I * blocks_a, span, channels), jnp.float32),
             pltpu.VMEM((regions, span, channels), jnp.float32),
             pltpu.VMEM((regions, steps_a, STRIPS, channels), jnp.float32),
-            pltpu.VMEM((2, groups, CHUNKS, WIDE, WIDE), jnp.bfloat16),
-            pltpu.VMEM((groups, blocks_a + 1, pairs_a + 3, STRIPS, WIDE), jnp.bfloat16),
-            pltpu.VMEM((groups, blocks_a, pairs_a, STRIPS, WIDE), jnp.bfloat16),
-            pltpu.VMEM((PHASE_I, pairs_a, STRIPS, 2 * channels), jnp.bfloat16),
+            pltpu.VMEM((groups, 2, blocks_a + 1, pairs_a + 3, STRIPS, LANES), jnp.bfloat16),
+            pltpu.VMEM((groups, 2, blocks_a, pairs_a, STRIPS, LANES), jnp.bfloat16),
+            pltpu.VMEM((PHASE_J, PHASE_I, pairs_a, STRIPS, channels), jnp.bfloat16),
             pltpu.VMEM((PHASE_I, width, channels), jnp.float32),
             pltpu.VMEM((WIDE, WIDE), jnp.bfloat16),
             pltpu.VMEM((WIDE, WIDE), jnp.bfloat16),
-            pltpu.SemaphoreType.DMA((2,)),
+            pltpu.VMEM((2, 2 * channels, weights[2].shape[2]), jnp.bfloat16),
+            pltpu.VMEM((2, weights[2].shape[2], channels), jnp.bfloat16),
         ],
-        compiler_params=pltpu.CompilerParams(vmem_limit_bytes=60 << 20),
+        compiler_params=pltpu.CompilerParams(vmem_limit_bytes=30 << 20),
         name="blocks",
     )(wet, state, top, bottom, west, east, *bands, *weights)
 
@@ -377,53 +469,15 @@
     outer_weight,
     outer_bias,
 ):
-    height, _, channels = ocean_field.shape
-    tile = height // wet_tiles.shape[0]
-    dtype = ocean_field.dtype
-
-    def rim_rows(edge, flags):
-        wet = jnp.repeat(flags, tile)[None, :, None]
-        kept = jnp.where(wet > 0, edge, jnp.zeros((), dtype))
-        return jnp.concatenate(
-            [kept, jnp.broadcast_to(wet, (1,) + edge.shape[1:]).astype(dtype)], axis=0
-        )
-
-    top, bottom = shift_pair(
-        rim_rows(ocean_field[:RIM], wet_tiles[0]),
-        rim_rows(ocean_field[-RIM:], wet_tiles[-1]),
-        "lon",
-        True,
-    )
-
-    def rim_cols(edge, flags, above, below):
-        wet = jnp.repeat(flags, tile)[:, None, None]
-        kept = jnp.where(wet > 0, edge, jnp.zeros((), dtype))
-        middle = jnp.concatenate(
-            [kept, jnp.broadcast_to(wet, (height, 1, channels)).astype(dtype)], axis=1
-        )
-        ends = [
-            jnp.concatenate(
-                [rim[:RIM], jnp.broadcast_to(rim[RIM:, :1], (RIM, 1, channels))], axis=1
-            )
-            for rim in (above, below)
-        ]
-        return jnp.concatenate([ends[0], middle, ends[1]], axis=0)
-
-    west, east = shift_pair(
-        rim_cols(ocean_field[:, :RIM], wet_tiles[:, 0], top[:, :RIM], bottom[:, :RIM]),
-        rim_cols(ocean_field[:, -RIM:], wet_tiles[:, -1], top[:, -RIM:], bottom[:, -RIM:]),
-        "lat",
-        False,
-    )
-    bands = [band_call(conv_weight[layer]) for layer in range(conv_weight.shape[0])]
-    weights = (
-        jnp.tile(norm_gain, (1, 2)),
-        jnp.tile(norm_bias, (1, 2)),
-        inner_weight,
-        inner_bias,
-        outer_weight,
-        outer_bias,
-    )
+    tile = ocean_field.shape[0] // wet_tiles.shape[0]
+    rows = rim_rows_call(wet_tiles, ocean_field, tile)
+    top, bottom = shift_pair(*rows, "lon", True)
+    cols = rim_cols_call(wet_tiles, ocean_field, top, bottom, tile)
+    west, east = shift_pair(*cols, "lat", False)
+    bands = []
+    for layer in range(conv_weight.shape[0]):
+        bands.append(band_call(conv_weight, layer))
+    weights = (norm_gain, norm_bias, inner_weight, inner_bias, outer_weight, outer_bias)
     return blocks_call(wet_tiles, ocean_field, top, bottom, west, east, bands, weights, tile)
 
 

time: 80 us -> 71.2 us (0.89)
  local copies, waits for them, and re-layouts: 11 us -> 2.31 us
  waiting for transfers between devices: 4.04 us -> 10.1 us
  other arithmetic: 3.6 us -> 0 us
  between operations: 2.77 us -> 0.21 us
    unnamed x16 -> x23, local copies, waits for them, and re-layouts: 7.81 us -> 2.31 us
    ppermute x2, waiting for transfers between devices: 0.01 us -> 5.24 us  [shift_pair(): lax.ppermute(tail, axis, [(i, (i + 1) % count) for i in range(ends)])]
    ppermute x2, starting transfers between devices: 4.05 us -> 6.7 us  [shift_pair(): lax.ppermute(tail, axis, [(i, (i + 1) % count) for i in range(ends)])]
    slice x4 -> x0, local copies, waits for them, and re-layouts: 2.2 us -> none  [the longest x1 1.32 us: per_device(): wet_tiles[:, 0]]
    select_n x2 -> x0, other arithmetic: 2.14 us -> none  [the longest x1 1.12 us: rim_rows(): kept = jnp.where(wet > 0, edge, jnp.zeros((), dtype))]
    ppermute x2, starting transfers between devices: 4.96 us -> 2.94 us  [shift_pair(): lax.ppermute(head, axis, [((i + 1) % count, i) for i in range(ends)])]
    pallas_call x1, Pallas kernels: 44.9 us -> 43 us  [blocks_call(): pl.pallas_call(functools.partial(blocks_body, tile=tile), out_shape=jax.S...]
    pallas_call x0 -> x2, Pallas kernels: none -> 1.26 us  [the longest x1 0.66 us: rim_cols_call(): pl.pallas_call(functools.partial(rim_cols_body, tile=tile), grid=(1,), ou...]
  transfers between devices with their start and end apart: 4 -> 4, of which waited for: 1 -> 2; matrix products, arithmetic and copies ran while one was open for 6% -> 0% of each run, Pallas kernels for 5% -> 6%
where the time goes in v3:
time: 71.2 us; the launch traced here: 71.1 us
  Pallas kernels  48.8 us (69%)
  waiting for transfers between devices  10.1 us (14%)
  starting transfers between devices  9.64 us (14%)
  local copies, waits for them, and re-layouts  2.31 us (3%)
    pallas_call x1, Pallas kernels, blocks_call(): pl.pallas_call(functools.partial(blocks_body, tile=tile), out_shape=jax.S...  43 us
    ppermute x2, starting transfers between devices, shift_pair(): lax.ppermute(tail, axis, [(i, (i + 1) % count) for i in range(ends)])  6.7 us
    ppermute x2, waiting for transfers between devices, shift_pair(): lax.ppermute(tail, axis, [(i, (i + 1) % count) for i in range(ends)])  5.24 us
    ppermute x2, waiting for transfers between devices, shift_pair(): lax.ppermute(head, axis, [((i + 1) % count, i) for i in range(ends)])  4.89 us
    pallas_call x2, Pallas kernels, band_call(): pl.pallas_call(band_body, grid=(groups,), out_shape=jax.ShapeDtypeStruct(...  4.49 us
    ppermute x2, starting transfers between devices, shift_pair(): lax.ppermute(head, axis, [((i + 1) % count, i) for i in range(ends)])  2.94 us
    unnamed x23, local copies, waits for them, and re-layouts  2.31 us
  transfers between devices with their start and end apart: 4, of which 2 were waited for; matrix products, arithmetic and copies ran while one was open for 0% of the time, Pallas kernels for 6%

profile of v3, /device:TPU:1, one launch (start us, length us, event | category | flops | bytes accessed | tf_op | source)
XLA Modules:
  0.0 71.1 jit_solution(4625841940028928032)
XLA Ops:
  0.0 1.6 %copy-done = bf16[64,128,128]{2,1,0:T(8,128)(2,1)S(1)} copy-done((bf16[64,128,128]{2,1,0:T(8,128)(2,1)S(1)}, bf16[64,128,128]{2,1,0:T(8,128)(2,1)}, u32[]{:S(2)}) %copy-start) | copy-done | bytes 2097176
  1.6 0.7 copy-done.4
  2.2 0.6 rim_rows.1
  2.9 2.1 %collective-permute-start = (bf16[7,128,128]{2,1,0:T(8,128)(2,1)S(1)}, bf16[7,128,128]{2,1,0:T(8,128)(2,1)S(1)}, u32[]{:S(2)}, u32[]{:S(2)}) collective-permute-start(bf16[7,128,128]{2,1,0:T(8,128)(2,1)S(1)} %get-tuple-element.9), channel_id=1, source_target_pairs={{0,8},{8,16},{16,24},{24,0},{1,9},{9,17},{17,25},{25,1},{2,10},{10... | collective-permute-start | bytes 688136 | tf_op jit(solution)/shard_map/ppermute | solution.py:456
  4.9 1.0 %collective-permute-start.1 = (bf16[7,128,128]{2,1,0:T(8,128)(2,1)S(1)}, bf16[7,128,128]{2,1,0:T(8,128)(2,1)S(1)}, u32[]{:S(2)}, u32[]{:S(2)}) collective-permute-start(bf16[7,128,128]{2,1,0:T(8,128)(2,1)S(1)} %get-tuple-element.10), channel_id=1, source_target_pairs={{8,0},{16,8},{24,16},{0,24},{9,1},{17,9},{25,17},{1,25},{10,2},{18... | collective-permute-start | bytes 688136 | tf_op jit(solution)/shard_map/ppermute | solution.py:457
  6.0 5.2 %collective-permute-done.top_ref = bf16[7,128,128]{2,1,0:T(8,128)(2,1)S(1)} collective-permute-done((bf16[7,128,128]{2,1,0:T(8,128)(2,1)S(1)}, bf16[7,128,128]{2,1,0:T(8,128)(2,1)S(1)}, u32[]{:S(2)}, u32[]{:S(2)}) %collective-permute-start) | collective-permute-done | bytes 229408 | tf_op jit(solution)/shard_map/ppermute | solution.py:456
  11.2 4.9 %collective-permute-done.1.bottom_ref = bf16[7,128,128]{2,1,0:T(8,128)(2,1)S(1)} collective-permute-done((bf16[7,128,128]{2,1,0:T(8,128)(2,1)S(1)}, bf16[7,128,128]{2,1,0:T(8,128)(2,1)S(1)}, u32[]{:S(2)}, u32[]{:S(2)}) %collective-permute-start.1) | collective-permute-done | bytes 229408 | tf_op jit(solution)/shard_map/ppermute | solution.py:457
  16.1 0.7 rim_cols.1
  16.8 4.6 %collective-permute-start.2 = (bf16[76,7,128]{2,1,0:T(8,128)(2,1)S(1)}, bf16[76,7,128]{2,1,0:T(8,128)(2,1)S(1)}, u32[]{:S(2)}, u32[]{:S(2)}) collective-permute-start(bf16[76,7,128]{2,1,0:T(8,128)(2,1)S(1)} %get-tuple-element.11), channel_id=1, source_target_pairs={{0,1},{1,2},{2,3},{3,4},{4,5},{5,6},{6,7},{8,9},{9,10},{10,11},{11... | collective-permute-start | bytes 408584 | tf_op jit(solution)/shard_map/ppermute | solution.py:456
  21.4 1.9 %collective-permute-start.3 = (bf16[76,7,128]{2,1,0:T(8,128)(2,1)S(1)}, bf16[76,7,128]{2,1,0:T(8,128)(2,1)S(1)}, u32[]{:S(2)}, u32[]{:S(2)}) collective-permute-start(bf16[76,7,128]{2,1,0:T(8,128)(2,1)S(1)} %get-tuple-element.12), channel_id=1, source_target_pairs={{1,0},{2,1},{3,2},{4,3},{5,4},{6,5},{7,6},{9,8},{10,9},{11,10},{12... | collective-permute-start | bytes 408584 | tf_op jit(solution)/shard_map/ppermute | solution.py:457
  23.3 0.0 copy-done.10
  23.3 0.0 copy-start.1
  23.4 0.0 copy-start.2
  23.4 0.0 copy-start.3
  23.4 0.0 copy-start.5
  23.4 0.0 copy-start.6
  23.4 0.0 copy-start.7
  23.4 0.0 copy-start.8
  23.4 0.0 copy-start.9
  23.4 2.2 %bands.3.band_b_ref = bf16[8,8,2,256,128]{4,3,2,1,0:T(8,128)(2,1)S(1)} custom-call(bf16[2,7,7,128]{3,2,1,0:T(8,128)(2,1)S(1)} %copy.10.conv_ref), custom_call_target="tpu_custom_call" | custom-call | flops 16777216 | bytes 8388608 | tf_op jit(solution)/shard_map/bands/pallas_call | solution.py:83
  25.7 2.2 %bands.2.band_a_ref = bf16[8,8,2,256,128]{4,3,2,1,0:T(8,128)(2,1)S(1)} custom-call(bf16[2,7,7,128]{3,2,1,0:T(8,128)(2,1)S(1)} %copy.10.conv_ref), custom_call_target="tpu_custom_call" | custom-call | flops 16777216 | bytes 8388608 | tf_op jit(solution)/shard_map/bands/pallas_call | solution.py:83
  27.9 0.0 collective-permute-done.2.west_ref
  28.0 0.0 collective-permute-done.3.east_ref
  28.0 0.0 copy-done.1
  28.0 0.0 copy-done.2
  28.0 0.0 copy-done.3
  28.0 0.0 copy-done.5
  28.0 0.0 copy-done.6
  28.0 0.0 copy-done.7
  28.0 0.0 copy-done.8
  28.0 0.0 copy-done.9
  28.0 43.0 %blocks.1 = bf16[64,128,128]{2,1,0:T(8,128)(2,1)} custom-call(s32[1,2]{1,0:T(1,128)S(1)} %copy-done.5, bf16[64,128,128]{2,1,0:T(8,128)(2,1)S(1)} %copy-done.1, bf16[7,128,128]{2,1,0:T(8,128)(2,1)S(1)} %collective-permute-done.top_ref, bf16[7,128,128]{2,1,0:T(8,128)(2,1)S(1)} %collective-permute-done.1.bottom_ref, ...), custom_call_target="tpu_custom_call" | custom-call | tf_op jit(solution)/shard_map/blocks/pallas_call | solution.py:429
  (4 shorter events, 0.0 us)
Async XLA Ops:
  0.0 1.6 %copy-start = (bf16[64,128,128]{2,1,0:T(8,128)(2,1)S(1)}, bf16[64,128,128]{2,1,0:T(8,128)(2,1)}, u32[]{:S(2)}) copy-start(bf16[64,128,128]{2,1,0:T(8,128)(2,1)} %state_ref.1) | copy-start | bytes 6291460
  1.6 0.7 copy-start.4
  2.2 21.1 %copy-start.10 = (bf16[2,7,7,128]{3,0,2,1:T(2,128)(2,1)S(1)}, bf16[2,7,7,128]{3,0,2,1:T(2,128)(2,1)}, u32[]{:S(2)}) copy-start(bf16[2,7,7,128]{3,0,2,1:T(2,128)(2,1)} %param.11) | copy-start | bytes 75268
  2.9 8.3 %collective-permute-start = (bf16[7,128,128]{2,1,0:T(8,128)(2,1)S(1)}, bf16[7,128,128]{2,1,0:T(8,128)(2,1)S(1)}, u32[]{:S(2)}, u32[]{:S(2)}) collective-permute-start(bf16[7,128,128]{2,1,0:T(8,128)(2,1)S(1)} %get-tuple-element.9), channel_id=1, source_target_pairs={{0,8},{8,16},{16,24},{24,0},{1,9},{9,17},{17,25},{25,1},{2,10},{10... | collective-permute-start | bytes 688136 | tf_op jit(solution)/shard_map/ppermute | solution.py:456
  4.9 11.1 %collective-permute-start.1 = (bf16[7,128,128]{2,1,0:T(8,128)(2,1)S(1)}, bf16[7,128,128]{2,1,0:T(8,128)(2,1)S(1)}, u32[]{:S(2)}, u32[]{:S(2)}) collective-permute-start(bf16[7,128,128]{2,1,0:T(8,128)(2,1)S(1)} %get-tuple-element.10), channel_id=1, source_target_pairs={{8,0},{16,8},{24,16},{0,24},{9,1},{17,9},{25,17},{1,25},{10,2},{18... | collective-permute-start | bytes 688136 | tf_op jit(solution)/shard_map/ppermute | solution.py:457
  16.8 11.2 %collective-permute-start.2 = (bf16[76,7,128]{2,1,0:T(8,128)(2,1)S(1)}, bf16[76,7,128]{2,1,0:T(8,128)(2,1)S(1)}, u32[]{:S(2)}, u32[]{:S(2)}) collective-permute-start(bf16[76,7,128]{2,1,0:T(8,128)(2,1)S(1)} %get-tuple-element.11), channel_id=1, source_target_pairs={{0,1},{1,2},{2,3},{3,4},{4,5},{5,6},{6,7},{8,9},{9,10},{10,11},{11... | collective-permute-start | bytes 408584 | tf_op jit(solution)/shard_map/ppermute | solution.py:456
  21.4 6.6 %collective-permute-start.3 = (bf16[76,7,128]{2,1,0:T(8,128)(2,1)S(1)}, bf16[76,7,128]{2,1,0:T(8,128)(2,1)S(1)}, u32[]{:S(2)}, u32[]{:S(2)}) collective-permute-start(bf16[76,7,128]{2,1,0:T(8,128)(2,1)S(1)} %get-tuple-element.12), channel_id=1, source_target_pairs={{1,0},{2,1},{3,2},{4,3},{5,4},{6,5},{7,6},{9,8},{10,9},{11,10},{12... | collective-permute-start | bytes 408584 | tf_op jit(solution)/shard_map/ppermute | solution.py:457
  23.3 4.6 %copy-start.1 = (bf16[64,128,128]{2,1,0:T(8,128)(2,1)S(1)}, bf16[64,128,128]{2,1,0:T(8,128)(2,1)}, u32[]{:S(2)}) copy-start(bf16[64,128,128]{2,1,0:T(8,128)(2,1)} %state_ref.1) | copy-start | bytes 6291460
  23.4 4.6 %copy-start.2 = (bf16[2,128,256]{2,1,0:T(8,128)(2,1)S(1)}, bf16[2,128,256]{2,1,0:T(8,128)(2,1)}, u32[]{:S(2)}) copy-start(bf16[2,128,256]{2,1,0:T(8,128)(2,1)} %inner_ref.1) | copy-start | bytes 393220
  23.4 4.6 %copy-start.3 = (bf16[2,256,128]{2,1,0:T(8,128)(2,1)S(1)}, bf16[2,256,128]{2,1,0:T(8,128)(2,1)}, u32[]{:S(2)}) copy-start(bf16[2,256,128]{2,1,0:T(8,128)(2,1)} %outer_ref.1) | copy-start | bytes 393220
  23.4 4.6 %copy-start.5 = (s32[1,2]{1,0:T(1,128)S(1)}, s32[1,2]{1,0:T(1,128)}, u32[]{:S(2)}) copy-start(s32[1,2]{1,0:T(1,128)} %wet_ref.5) | copy-start | bytes 28
  23.4 4.6 %copy-start.6 = (f32[2,256]{1,0:T(2,128)S(1)}, f32[2,256]{1,0:T(2,128)}, u32[]{:S(2)}) copy-start(f32[2,256]{1,0:T(2,128)} %inner_bias_ref.1) | copy-start | bytes 6148
  23.4 4.6 %copy-start.7 = (f32[2,128]{1,0:T(2,128)S(1)}, f32[2,128]{1,0:T(2,128)}, u32[]{:S(2)}) copy-start(f32[2,128]{1,0:T(2,128)} %gain_ref.1) | copy-start | bytes 3076
  23.4 4.6 %copy-start.8 = (f32[2,128]{1,0:T(2,128)S(1)}, f32[2,128]{1,0:T(2,128)}, u32[]{:S(2)}) copy-start(f32[2,128]{1,0:T(2,128)} %bias_ref.1) | copy-start | bytes 3076
  23.4 4.6 %copy-start.9 = (f32[2,128]{1,0:T(2,128)S(1)}, f32[2,128]{1,0:T(2,128)}, u32[]{:S(2)}) copy-start(f32[2,128]{1,0:T(2,128)} %outer_bias_ref.1) | copy-start | bytes 3076

commit v4 on v3

--- a/solution.py
+++ b/solution.py
@@ -200,9 +200,6 @@
     second_ref,
     mask_ref,
     wets_ref,
-    phased_ref,
-    grouped_ref,
-    cells_ref,
     branch_ref,
     average_ref,
     center_ref,
@@ -210,6 +207,10 @@
     outer_half_ref,
     *,
     tile,
+    phased_ref,
+    grouped_ref,
+    cells_ref,
+    normed_ref,
 ):
     height, width, channels = state_ref.shape
     groups = channels // SEG
@@ -335,9 +336,9 @@
                 ].reshape(blocks, pairs, STRIPS, LANES)
             return carry
 
-        lax.fori_loop(0, groups, convolve, 0)
-
-        def mix(blk, carry):
+        lax.fori_loop(0, groups, convolve, 0, unroll=4)
+
+        def to_cells(blk):
             for v in range(pairs):
                 for half in range(2):
                     parts = swap_segments(
@@ -346,7 +347,10 @@
                     for p in range(8):
                         pi, pj = (half * 8 + p) // 2, (half * 8 + p) % 2
                         cells_ref[pj, pi, v] = parts[p]
-            count = PHASE_I * pairs * STRIPS
+
+        count = PHASE_I * pairs * STRIPS
+
+        def normalize():
             conv = jnp.concatenate(
                 [cells_ref[pj, :, 0:pairs].reshape(count, channels) for pj in range(PHASE_J)],
                 axis=1,
@@ -355,15 +359,30 @@
             var = jnp.dot(
                 (centered * centered).astype(bf16), average_ref[...], preferred_element_type=f32
             )
-            normed = (
-                centered * lax.rsqrt(var + 1e-06) * gain
-                + shift
-            ).astype(bf16)
+            normed = (centered * lax.rsqrt(var + 1e-06) * gain + shift).astype(bf16)
+            for pj in range(PHASE_J):
+                normed_ref[pj, 0:count] = normed[:, pj * channels : (pj + 1) * channels]
+
+        def finish(blk):
+            for pi in range(PHASE_I):
+                i = blk * PHASE_I + pi
+                for s in range(0, STRIPS, 2):
+                    wet = wet_ref[i // tile, s * steps // tile] > 0
+                    delta = jnp.concatenate(
+                        [branch_ref[pi, pl.ds(s + k, steps, stride=STRIPS), :] for k in range(2)],
+                        axis=0,
+                    )
+                    base = second_ref[i + REACH, LEFT + s * steps : LEFT + (s + 2) * steps, :]
+                    out_ref[i, s * steps : (s + 2) * steps, :] = jnp.where(
+                        wet, base + delta, 0.0
+                    ).astype(bf16)
+
+        def mix(blk, carry):
+            if index == 1:
+                finish(jnp.maximum(blk - 1, 0))
             for pj in range(PHASE_J):
                 pre = jnp.dot(
-                    jnp.concatenate(
-                        [normed[:, pj * channels : (pj + 1) * channels], bias_lanes], axis=1
-                    ),
+                    jnp.concatenate([normed_ref[pj, 0:count], bias_lanes], axis=1),
                     inner_wide_ref[index],
                     preferred_element_type=f32,
                 )
@@ -388,27 +407,16 @@
                             ) * wets_ref[region, t]
                         else:
                             branch_ref[pi, t * STRIPS : (t + 1) * STRIPS, :] = branch[pi, v]
-            if index == 1:
-                for pi in range(PHASE_I):
-                    i = blk * PHASE_I + pi
-                    for s in range(0, STRIPS, 2):
-                        wet = wet_ref[i // tile, s * steps // tile] > 0
-                        delta = jnp.concatenate(
-                            [
-                                branch_ref[pi, pl.ds(s + k, steps, stride=STRIPS), :]
-                                for k in range(2)
-                            ],
-                            axis=0,
-                        )
-                        base = second_ref[
-                            i + REACH, LEFT + s * steps : LEFT + (s + 2) * steps, :
-                        ]
-                        out_ref[i, s * steps : (s + 2) * steps, :] = jnp.where(
-                            wet, base + delta, 0.0
-                        ).astype(bf16)
+            normalize()
+            to_cells(jnp.minimum(blk + 2, blocks - 1))
             return carry
 
+        to_cells(0)
+        normalize()
+        to_cells(1)
         lax.fori_loop(0, blocks, mix, 0)
+        if index == 1:
+            finish(blocks - 1)
 
     layer(0, first_ref, band_a_ref, LEFT - RIM, blocks_a, steps_a)
     layer(1, second_ref, band_b_ref, LEFT - REACH, blocks_b, steps_b)
@@ -426,8 +434,18 @@
     assert channels == LANES and steps_b == 8 and height % PHASE_I == 0
     vmem = pl.BlockSpec(memory_space=pltpu.VMEM)
     smem = pl.BlockSpec(memory_space=pltpu.SMEM)
+    packed = dict(
+        phased_ref=pltpu.VMEM((groups, 2, blocks_a + 1, pairs_a + 3, STRIPS, LANES), jnp.bfloat16),
+        grouped_ref=pltpu.VMEM((groups, 2, blocks_a, pairs_a, STRIPS, LANES), jnp.bfloat16),
+        cells_ref=pltpu.VMEM((PHASE_J, PHASE_I, pairs_a, STRIPS, channels), jnp.bfloat16),
+        normed_ref=pltpu.VMEM((PHASE_J, PHASE_I * pairs_a * STRIPS, channels), jnp.bfloat16),
+    )
+
+    def body(*refs):
+        pl.run_scoped(functools.partial(blocks_body, *refs, tile=tile), **packed)
+
     return pl.pallas_call(
-        functools.partial(blocks_body, tile=tile),
+        body,
         out_shape=jax.ShapeDtypeStruct(state.shape, jnp.bfloat16),
         in_specs=[smem] + [vmem] * 13,
         out_specs=vmem,
@@ -436,9 +454,6 @@
             pltpu.VMEM((PHASE_I * blocks_a, span, channels), jnp.float32),
             pltpu.VMEM((regions, span, channels), jnp.float32),
             pltpu.VMEM((regions, steps_a, STRIPS, channels), jnp.float32),
-            pltpu.VMEM((groups, 2, blocks_a + 1, pairs_a + 3, STRIPS, LANES), jnp.bfloat16),
-            pltpu.VMEM((groups, 2, blocks_a, pairs_a, STRIPS, LANES), jnp.bfloat16),
-            pltpu.VMEM((PHASE_J, PHASE_I, pairs_a, STRIPS, channels), jnp.bfloat16),
             pltpu.VMEM((PHASE_I, width, channels), jnp.float32),
             pltpu.VMEM((WIDE, WIDE), jnp.bfloat16),
             pltpu.VMEM((WIDE, WIDE), jnp.bfloat16),

time: 71.2 us -> 65.1 us (0.914)
  Pallas kernels: 48.8 us -> 42.7 us
    pallas_call x1, Pallas kernels: 43 us -> 36.9 us  [blocks_call(): pl.pallas_call(body, out_shape=jax.ShapeDtypeStruct(state.shape, jnp.bflo...]
  transfers between devices with their start and end apart: 4 -> 4, of which waited for: 2 -> 2; matrix products, arithmetic and copies ran while one was open for 0% -> 0% of each run, Pallas kernels for 6% -> 7%
where the time goes in v4:
time: 65.1 us; the launch traced here: 64.9 us
  Pallas kernels  42.7 us (66%)
  waiting for transfers between devices  10.1 us (16%)
  starting transfers between devices  9.64 us (15%)
  local copies, waits for them, and re-layouts  2.31 us (4%)
    pallas_call x1, Pallas kernels, blocks_call(): pl.pallas_call(body, out_shape=jax.ShapeDtypeStruct(state.shape, jnp.bflo...  36.9 us
    ppermute x2, starting transfers between devices, shift_pair(): lax.ppermute(tail, axis, [(i, (i + 1) % count) for i in range(ends)])  6.7 us
    ppermute x2, waiting for transfers between devices, shift_pair(): lax.ppermute(tail, axis, [(i, (i + 1) % count) for i in range(ends)])  5.24 us
    ppermute x2, waiting for transfers between devices, shift_pair(): lax.ppermute(head, axis, [((i + 1) % count, i) for i in range(ends)])  4.89 us
    pallas_call x2, Pallas kernels, band_call(): pl.pallas_call(band_body, grid=(groups,), out_shape=jax.ShapeDtypeStruct(...  4.49 us
    ppermute x2, starting transfers between devices, shift_pair(): lax.ppermute(head, axis, [((i + 1) % count, i) for i in range(ends)])  2.94 us
    unnamed x23, local copies, waits for them, and re-layouts  2.31 us
  transfers between devices with their start and end apart: 4, of which 2 were waited for; matrix products, arithmetic and copies ran while one was open for 0% of the time, Pallas kernels for 7%

profile of v4, /device:TPU:1, one launch (start us, length us, event | category | flops | bytes accessed | tf_op | source)
XLA Modules:
  0.0 64.9 jit_solution(11799182504220674533)
XLA Ops:
  0.0 1.6 %copy-done = bf16[64,128,128]{2,1,0:T(8,128)(2,1)S(1)} copy-done((bf16[64,128,128]{2,1,0:T(8,128)(2,1)S(1)}, bf16[64,128,128]{2,1,0:T(8,128)(2,1)}, u32[]{:S(2)}) %copy-start) | copy-done | bytes 2097176
  1.6 0.7 %copy-done.4 = s32[1,2]{1,0:T(1,128)S(1)} copy-done((s32[1,2]{1,0:T(1,128)S(1)}, s32[1,2]{1,0:T(1,128)}, u32[]{:S(2)}) %copy-start.4) | copy-done | bytes 32
  2.2 0.6 rim_rows.1
  2.9 2.1 %collective-permute-start = (bf16[7,128,128]{2,1,0:T(8,128)(2,1)S(1)}, bf16[7,128,128]{2,1,0:T(8,128)(2,1)S(1)}, u32[]{:S(2)}, u32[]{:S(2)}) collective-permute-start(bf16[7,128,128]{2,1,0:T(8,128)(2,1)S(1)} %get-tuple-element.9), channel_id=1, source_target_pairs={{0,8},{8,16},{16,24},{24,0},{1,9},{9,17},{17,25},{25,1},{2,10},{10... | collective-permute-start | bytes 688136 | tf_op jit(solution)/shard_map/ppermute | solution.py:471
  4.9 1.0 %collective-permute-start.1 = (bf16[7,128,128]{2,1,0:T(8,128)(2,1)S(1)}, bf16[7,128,128]{2,1,0:T(8,128)(2,1)S(1)}, u32[]{:S(2)}, u32[]{:S(2)}) collective-permute-start(bf16[7,128,128]{2,1,0:T(8,128)(2,1)S(1)} %get-tuple-element.10), channel_id=1, source_target_pairs={{8,0},{16,8},{24,16},{0,24},{9,1},{17,9},{25,17},{1,25},{10,2},{18... | collective-permute-start | bytes 688136 | tf_op jit(solution)/shard_map/ppermute | solution.py:472
  6.0 5.2 %collective-permute-done.top_ref.refs_2_ = bf16[7,128,128]{2,1,0:T(8,128)(2,1)S(1)} collective-permute-done((bf16[7,128,128]{2,1,0:T(8,128)(2,1)S(1)}, bf16[7,128,128]{2,1,0:T(8,128)(2,1)S(1)}, u32[]{:S(2)}, u32[]{:S(2)}) %collective-permute-start) | collective-permute-done | bytes 229408 | tf_op jit(solution)/shard_map/ppermute | solution.py:471
  11.2 4.9 %collective-permute-done.1.bottom_ref.refs_3_ = bf16[7,128,128]{2,1,0:T(8,128)(2,1)S(1)} collective-permute-done((bf16[7,128,128]{2,1,0:T(8,128)(2,1)S(1)}, bf16[7,128,128]{2,1,0:T(8,128)(2,1)S(1)}, u32[]{:S(2)}, u32[]{:S(2)}) %collective-permute-start.1) | collective-permute-done | bytes 229408 | tf_op jit(solution)/shard_map/ppermute | solution.py:472
  16.1 0.7 %rim_cols.1 = (bf16[76,7,128]{2,1,0:T(8,128)(2,1)S(1)}, bf16[76,7,128]{2,1,0:T(8,128)(2,1)S(1)}) custom-call(s32[1,2]{1,0:T(1,128)S(1)} %copy-done.4, bf16[64,128,128]{2,1,0:T(8,128)(2,1)S(1)} %copy-done, bf16[64,128,128]{2,1,0:T(8,128)(2,1)S(1)} %copy-done, bf16[7,128,128]{2,1,0:T(8,128)(2,1)S(1)} %collective-permute-done.top_ref.refs_2_, ...), custom_call_target="tpu_custom_call" | custom-call | tf_op jit(solution)/shard_map/rim_cols/pallas_call | solution.py:166
  16.8 4.6 %collective-permute-start.2 = (bf16[76,7,128]{2,1,0:T(8,128)(2,1)S(1)}, bf16[76,7,128]{2,1,0:T(8,128)(2,1)S(1)}, u32[]{:S(2)}, u32[]{:S(2)}) collective-permute-start(bf16[76,7,128]{2,1,0:T(8,128)(2,1)S(1)} %get-tuple-element.11), channel_id=1, source_target_pairs={{0,1},{1,2},{2,3},{3,4},{4,5},{5,6},{6,7},{8,9},{9,10},{10,11},{11... | collective-permute-start | bytes 408584 | tf_op jit(solution)/shard_map/ppermute | solution.py:471
  21.4 1.9 %collective-permute-start.3 = (bf16[76,7,128]{2,1,0:T(8,128)(2,1)S(1)}, bf16[76,7,128]{2,1,0:T(8,128)(2,1)S(1)}, u32[]{:S(2)}, u32[]{:S(2)}) collective-permute-start(bf16[76,7,128]{2,1,0:T(8,128)(2,1)S(1)} %get-tuple-element.12), channel_id=1, source_target_pairs={{1,0},{2,1},{3,2},{4,3},{5,4},{6,5},{7,6},{9,8},{10,9},{11,10},{12... | collective-permute-start | bytes 408584 | tf_op jit(solution)/shard_map/ppermute | solution.py:472
  23.3 0.0 copy-done.10
  23.3 0.0 copy-start.1
  23.4 0.0 copy-start.2
  23.4 0.0 copy-start.3
  23.4 0.0 copy-start.5
  23.4 0.0 copy-start.6
  23.4 0.0 copy-start.7
  23.4 0.0 copy-start.8
  23.4 0.0 copy-start.9
  23.4 2.2 %bands.3.refs_7_ = bf16[8,8,2,256,128]{4,3,2,1,0:T(8,128)(2,1)S(1)} custom-call(bf16[2,7,7,128]{3,2,1,0:T(8,128)(2,1)S(1)} %copy.10.conv_ref), custom_call_target="tpu_custom_call" | custom-call | flops 16777216 | bytes 8388608 | tf_op jit(solution)/shard_map/bands/pallas_call | solution.py:83
  25.7 2.2 %bands.2.refs_6_ = bf16[8,8,2,256,128]{4,3,2,1,0:T(8,128)(2,1)S(1)} custom-call(bf16[2,7,7,128]{3,2,1,0:T(8,128)(2,1)S(1)} %copy.10.conv_ref), custom_call_target="tpu_custom_call" | custom-call | flops 16777216 | bytes 8388608 | tf_op jit(solution)/shard_map/bands/pallas_call | solution.py:83
  27.9 0.0 collective-permute-done.2.refs_4_
  28.0 0.0 collective-permute-done.3.refs_5_
  28.0 0.0 copy-done.1
  28.0 0.0 copy-done.2
  28.0 0.0 copy-done.3
  28.0 0.0 copy-done.5
  28.0 0.0 copy-done.6
  28.0 0.0 copy-done.7
  28.0 0.0 copy-done.8
  28.0 0.0 copy-done.9
  28.0 36.9 %blocks.1 = bf16[64,128,128]{2,1,0:T(8,128)(2,1)} custom-call(s32[1,2]{1,0:T(1,128)S(1)} %copy-done.5, bf16[64,128,128]{2,1,0:T(8,128)(2,1)S(1)} %copy-done.1, bf16[7,128,128]{2,1,0:T(8,128)(2,1)S(1)} %collective-permute-done.top_ref.refs_2_, bf16[7,128,128]{2,1,0:T(8,128)(2,1)S(1)} %collective-permute-done.1.bottom_ref.refs_3_, ...), custom_call_target="tpu_custom_call" | custom-call | tf_op jit(solution)/shard_map/blocks/pallas_call | solution.py:447
  (4 shorter events, 0.0 us)
Async XLA Ops:
  0.0 1.6 %copy-start = (bf16[64,128,128]{2,1,0:T(8,128)(2,1)S(1)}, bf16[64,128,128]{2,1,0:T(8,128)(2,1)}, u32[]{:S(2)}) copy-start(bf16[64,128,128]{2,1,0:T(8,128)(2,1)} %refs_1_.1) | copy-start | bytes 6291460
  1.6 0.7 %copy-start.4 = (s32[1,2]{1,0:T(1,128)S(1)}, s32[1,2]{1,0:T(1,128)}, u32[]{:S(2)}) copy-start(s32[1,2]{1,0:T(1,128)} %refs_0_.1) | copy-start | bytes 28
  2.2 21.1 %copy-start.10 = (bf16[2,7,7,128]{3,0,2,1:T(2,128)(2,1)S(1)}, bf16[2,7,7,128]{3,0,2,1:T(2,128)(2,1)}, u32[]{:S(2)}) copy-start(bf16[2,7,7,128]{3,0,2,1:T(2,128)(2,1)} %param.11) | copy-start | bytes 75268
  2.9 8.3 %collective-permute-start = (bf16[7,128,128]{2,1,0:T(8,128)(2,1)S(1)}, bf16[7,128,128]{2,1,0:T(8,128)(2,1)S(1)}, u32[]{:S(2)}, u32[]{:S(2)}) collective-permute-start(bf16[7,128,128]{2,1,0:T(8,128)(2,1)S(1)} %get-tuple-element.9), channel_id=1, source_target_pairs={{0,8},{8,16},{16,24},{24,0},{1,9},{9,17},{17,25},{25,1},{2,10},{10... | collective-permute-start | bytes 688136 | tf_op jit(solution)/shard_map/ppermute | solution.py:471
  4.9 11.1 %collective-permute-start.1 = (bf16[7,128,128]{2,1,0:T(8,128)(2,1)S(1)}, bf16[7,128,128]{2,1,0:T(8,128)(2,1)S(1)}, u32[]{:S(2)}, u32[]{:S(2)}) collective-permute-start(bf16[7,128,128]{2,1,0:T(8,128)(2,1)S(1)} %get-tuple-element.10), channel_id=1, source_target_pairs={{8,0},{16,8},{24,16},{0,24},{9,1},{17,9},{25,17},{1,25},{10,2},{18... | collective-permute-start | bytes 688136 | tf_op jit(solution)/shard_map/ppermute | solution.py:472
  16.8 11.2 %collective-permute-start.2 = (bf16[76,7,128]{2,1,0:T(8,128)(2,1)S(1)}, bf16[76,7,128]{2,1,0:T(8,128)(2,1)S(1)}, u32[]{:S(2)}, u32[]{:S(2)}) collective-permute-start(bf16[76,7,128]{2,1,0:T(8,128)(2,1)S(1)} %get-tuple-element.11), channel_id=1, source_target_pairs={{0,1},{1,2},{2,3},{3,4},{4,5},{5,6},{6,7},{8,9},{9,10},{10,11},{11... | collective-permute-start | bytes 408584 | tf_op jit(solution)/shard_map/ppermute | solution.py:471
  21.4 6.6 %collective-permute-start.3 = (bf16[76,7,128]{2,1,0:T(8,128)(2,1)S(1)}, bf16[76,7,128]{2,1,0:T(8,128)(2,1)S(1)}, u32[]{:S(2)}, u32[]{:S(2)}) collective-permute-start(bf16[76,7,128]{2,1,0:T(8,128)(2,1)S(1)} %get-tuple-element.12), channel_id=1, source_target_pairs={{1,0},{2,1},{3,2},{4,3},{5,4},{6,5},{7,6},{9,8},{10,9},{11,10},{12... | collective-permute-start | bytes 408584 | tf_op jit(solution)/shard_map/ppermute | solution.py:472
  23.3 4.6 %copy-start.1 = (bf16[64,128,128]{2,1,0:T(8,128)(2,1)S(1)}, bf16[64,128,128]{2,1,0:T(8,128)(2,1)}, u32[]{:S(2)}) copy-start(bf16[64,128,128]{2,1,0:T(8,128)(2,1)} %refs_1_.1) | copy-start | bytes 6291460
  23.4 4.6 %copy-start.2 = (bf16[2,128,256]{2,1,0:T(8,128)(2,1)S(1)}, bf16[2,128,256]{2,1,0:T(8,128)(2,1)}, u32[]{:S(2)}) copy-start(bf16[2,128,256]{2,1,0:T(8,128)(2,1)} %refs_10_.1) | copy-start | bytes 393220
  23.4 4.6 %copy-start.3 = (bf16[2,256,128]{2,1,0:T(8,128)(2,1)S(1)}, bf16[2,256,128]{2,1,0:T(8,128)(2,1)}, u32[]{:S(2)}) copy-start(bf16[2,256,128]{2,1,0:T(8,128)(2,1)} %refs_12_.1) | copy-start | bytes 393220
  23.4 4.6 %copy-start.5 = (s32[1,2]{1,0:T(1,128)S(1)}, s32[1,2]{1,0:T(1,128)}, u32[]{:S(2)}) copy-start(s32[1,2]{1,0:T(1,128)} %refs_0_.1) | copy-start | bytes 28
  23.4 4.6 %copy-start.6 = (f32[2,256]{1,0:T(2,128)S(1)}, f32[2,256]{1,0:T(2,128)}, u32[]{:S(2)}) copy-start(f32[2,256]{1,0:T(2,128)} %refs_11_.1) | copy-start | bytes 6148
  23.4 4.6 %copy-start.7 = (f32[2,128]{1,0:T(2,128)S(1)}, f32[2,128]{1,0:T(2,128)}, u32[]{:S(2)}) copy-start(f32[2,128]{1,0:T(2,128)} %refs_8_.1) | copy-start | bytes 3076
  23.4 4.6 %copy-start.8 = (f32[2,128]{1,0:T(2,128)S(1)}, f32[2,128]{1,0:T(2,128)}, u32[]{:S(2)}) copy-start(f32[2,128]{1,0:T(2,128)} %refs_9_.1) | copy-start | bytes 3076
  23.4 4.6 %copy-start.9 = (f32[2,128]{1,0:T(2,128)S(1)}, f32[2,128]{1,0:T(2,128)}, u32[]{:S(2)}) copy-start(f32[2,128]{1,0:T(2,128)} %refs_13_.1) | copy-start | bytes 3076
